TPU v7x, 256 devices: a whole 4x4x8 slice. The times are simulated.
256 devices in a mesh: gx: 16 (over x_lo, z), ma: 16 (over y, x_hi, core).
Axes of the slice: x: 4 (x_hi: 2, x_lo: 2; x = x_hi * 2 + x_lo), y: 4, z: 8, core: 2. Of those that a mesh axis runs over, the one named last changes fastest.
Arguments:
- solution: float32 [256, 16, 8, 256], P('ma', 'gx'), may hold values from -1.2 to 1.2
- source: float32 [256, 16, 8, 256], P('ma', 'gx'), may hold values from -6 to 6
- mean_conductivity: float32 [16, 8, 256], P('gx'), may hold values from 0.5 to 2
- kl_fields: float32 [10, 16, 8, 256], P(None, 'gx'), may hold values from -0.9 to 0.9
- couplings: int32 [10, 256, 2], replicated, may hold values from 0 to 255, as said below
- mode_index: int32 [256, 10], replicated, may hold values from 0 to 3, as said below
Outputs:
- residual: float32 [256, 16, 8, 256], P('ma', 'gx')
- correction: float32 [256, 16, 8, 256], P('ma', 'gx')
Inputs may be any that keep to these rules, and one draw needn't show every extreme that they name: couplings[k, i, 0] is the mode whose multi-index is mode_index[i] plus one in variable k, couplings[k, i, 1] the mode whose multi-index is mode_index[i] minus one in variable k; where no mode has that multi-index the entry is i itself. `mode_index`: the rows are 256 distinct multi-indices of total degree at most 3 in graded order: the total degree never falls with the mode number, all multi-indices of each total degree below 3 are present, and some mode has degree 3 in one variable; the order of the variables is drawn from the seed.
All inputs are finite; a program needn't handle non-finite values.
Results may differ from a plain program's by a relative error of at most 0.000071.
Values sent between devices are 32-bit elements; how exact they have to be, the bound alone decides.
No kernel may reach another device: no remote copies, remote signals or barrier semaphores. Data moves between devices by JAX's collectives and lax.ppermute only.
A program may use at most 128 MiB of HBM per device.

v0:
```python
import jax
import jax.numpy as jnp
from jax import lax
from jax.sharding import PartitionSpec as P

STEPS = 3


def extended(array, sides, width):
    for axis, dim in sides:
        size, length = (lax.axis_size(axis), array.shape[dim])
        up = [(i, (i + 1) % size) for i in range(size)]
        down = [(j, i) for i, j in up]
        last = lax.slice_in_dim(array, length - width, length, axis=dim)
        initial = lax.slice_in_dim(array, 0, width, axis=dim)
        before = lax.ppermute(last, axis, up)
        after = lax.ppermute(initial, axis, down)
        array = jnp.concatenate([before, array, after], axis=dim)
    return array


def diffuse(coefficient, padded):
    center = coefficient[1:-1]
    values = padded[..., 1:-1, :, :]
    total = 0.5 * (center + coefficient[2:]) * (values - padded[..., 2:, :, :])
    total = total + 0.5 * (center + coefficient[:-2]) * (values - padded[..., :-2, :, :])
    for which_dim in (-2, -1):
        for offset in (-1, 1):
            total = total + 0.5 * (center + jnp.roll(center, offset, which_dim)) * (
                values - jnp.roll(values, offset, which_dim)
            )
    return total


def coupling_table(couplings, mode_index):
    modes_all = mode_index.shape[0]
    degrees = mode_index.astype(jnp.float32).T
    weight = jnp.sqrt(jnp.maximum(degrees[:, :, None], degrees[:, None, :]))
    columns = lax.broadcasted_iota(jnp.int32, (1, 1, 1, modes_all), 3)
    counted = jnp.sum((couplings[..., None] == columns).astype(jnp.float32), axis=2)
    row_ids = lax.broadcasted_iota(jnp.int32, (1, modes_all, modes_all), 1)
    col_ids = lax.broadcasted_iota(jnp.int32, (1, modes_all, modes_all), 2)
    off_diagonal = (row_ids != col_ids).astype(jnp.float32)
    return counted * weight * off_diagonal


def shards(solution, source, mean_conductivity, kl_fields, couplings, mode_index):
    modes_here = solution.shape[0]
    fields = kl_fields.shape[0]
    shape = solution.shape
    cells = shape[1] * shape[2] * shape[3]
    block_start = lax.axis_index("ma") * modes_here
    g_full = coupling_table(couplings, mode_index)
    g_rows = lax.dynamic_slice_in_dim(g_full, block_start, modes_here, 1)
    stacked = jnp.concatenate([mean_conductivity[None], kl_fields], 0)
    padded_fields = extended(stacked, (("gx", 1),), 1)
    mean_pad = padded_fields[0]
    kl_pad = padded_fields[1:]
    padded_solution = extended(solution, (("gx", 1),), 1)
    image = solution + diffuse(mean_pad, padded_solution)
    piece = lax.all_gather(padded_solution, "ma", axis=0, tiled=True)
    count = piece.shape[0]
    terms = jnp.stack([diffuse(kl_pad[field_id], piece) for field_id in range(fields)])
    terms = terms.reshape(fields, count, cells)
    coupled = jnp.einsum("kij,kjc->ic", g_rows, terms, precision=lax.Precision.HIGHEST)
    image = image + coupled.reshape(shape)
    residual = source - image
    theta = 13.0
    delta = 12.0
    sigma = theta / delta
    rho = 1.0 / sigma
    direction = residual / theta
    correction = direction
    remain = residual
    for step in range(STEPS):
        padded_direction = extended(direction, (("gx", 1),), 1)
        applied = direction + diffuse(mean_pad, padded_direction)
        remain = remain - applied
        rho_next = 1.0 / (2.0 * sigma - rho)
        direction = rho_next * rho * direction + 2.0 * rho_next / delta * remain
        correction = correction + direction
        rho = rho_next
    return (residual, correction)


def solution(mesh):
    in_specs = (
        P("ma", "gx", None, None),
        P("ma", "gx", None, None),
        P("gx", None, None),
        P(None, "gx", None, None),
        P(),
        P(),
    )
    out_specs = (P("ma", "gx", None, None), P("ma", "gx", None, None))
    return jax.shard_map(shards, mesh=mesh, in_specs=in_specs, out_specs=out_specs, check_vma=False)
```

profile of v0, /device:TPU:2, one launch (start us, length us, event | category | flops | bytes accessed | tf_op | source)
XLA Modules:
  0.0 236.9 jit_solution(6606500784124083350)
XLA Ops:
  8.2 5.9 %collective-permute-start.1 = (f32[16,1,8,256]{3,0,2,1:T(8,128)S(1)}, f32[16,1,8,256]{3,0,2,1:T(8,128)S(1)}, u32[]{:S(2)}, u32[]{:S(2)}) collective-permute-start(f32[16,1,8,256]{3,0,2,1:T(8,128)S(1)} %copy.125), channel_id=1, source_target_pairs={{16,0},{32,16},{48,32},{64,48},{80,64},{96,80},{112,96},{128,112},... | collective-permute-start | bytes 393224 | tf_op jit(solution)/shard_map/ppermute | solution.py:17
  16.9 4.3 %collective-permute-done.3 = f32[16,1,8,256]{3,0,2,1:T(8,128)S(1)} collective-permute-done((f32[16,1,8,256]{3,0,2,1:T(8,128)S(1)}, f32[16,1,8,256]{3,0,2,1:T(8,128)S(1)}, u32[]{:S(2)}, u32[]{:S(2)}) %collective-permute-start.3) | collective-permute-done | bytes 131104 | tf_op jit(solution)/shard_map/ppermute | solution.py:16
  25.6 4.0 %convert_reduce_fusion = f32[10,256,256]{2,1,0:T(8,128)} fusion(s32[10,256,2]{1,2,0:T(2,128)} %param.10), kind=kLoop, calls=%fused_computation | loop fusion | flops 3276800 | bytes 2641920 | tf_op jit(solution)/shard_map/reduce_sum | solution.py:40
  41.9 45.2 %all-gather.2.cloned.1.call-done = f32[256,3,8,256]{3,0,2,1:T(8,128)} async-done(((f32[16,3,8,256]{3,0,2,1:T(8,128)}), f32[256,3,8,256]{3,0,2,1:T(8,128)}) %all-gather.2.cloned.1.call-update) | async-done | bytes 6291472 | tf_op jit(solution)/shard_map/all_gather | solution.py:61
  87.1 4.4 %fusion.185 = (f32[256,1,8,255]{3,0,2,1:T(8,128)S(1)}, f32[256,1,8,255]{3,0,2,1:T(8,128)}) fusion(f32[256,3,8,256]{3,0,2,1:T(8,128)} %all-gather.2.cloned.1.call-done), kind=kLoop, calls=%fused_computation.401 | loop fusion | bytes 8355840 | tf_op jit(solution)/shard_map/jit(_roll_static)/slice | solution.py:30
  94.6 5.4 %multiply_add_fusion = (f32[256,1,8,256]{3,0,2,1:T(8,128)}, f32[256,1,8,256]{3,0,2,1:T(8,128)S(1)}, f32[256,1,8,256]{3,0,2,1:T(8,128)S(1)}, f32[256,1,8,256]{3,0...) fusion(f32[8,256]{1,0:T(8,128)S(1)} %copy-done.93, ...), kind=kLoop, calls=%fused_computation.8 | loop fusion | flops 11010048 | bytes 29409280 | tf_op jit(solution)/shard_map/add | solution.py:29
  100.1 4.4 %multiply_add_fusion.1 = (f32[256,1,8,256]{3,0,2,1:T(8,128)}, f32[256,1,8,256]{3,0,2,1:T(8,128)}) fusion(f32[256,1,8,256]{3,0,2,1:T(8,128)S(1)} %get-tuple-element.18, f32[256,1,8,256]{3,0,2,1:T(8,128)S(1)} %get-tuple-element.17, f32[256,1,8,256]{3,0,2,1:T(8,128)S(1)} %get-tuple-element.16, f32[256,1,8,256]{3,0,2,1:T(8,128)S(1)} %get-tuple-element.15, ...), kind=kLoop, calls=%fused_computation.9 | loop fusion | flops 11534336 | bytes 16875520 | tf_op jit(solution)/shard_map/add | solution.py:29
  105.2 3.1 %copy.150 = f32[256,1,8,256]{0,3,2,1:T(8,128)} copy(f32[256,1,8,256]{3,0,2,1:T(8,128)} %get-tuple-element.20) | data formatting | bytes 4194304 | tf_op jit(solution)/shard_map/add | solution.py:29
  108.4 6.5 %multiply_add_fusion.3 = (f32[256,1,8,256]{3,0,2,1:T(8,128)}, f32[256,1,8,256]{3,0,2,1:T(8,128)}) fusion(f32[256,1,8,256]{3,0,2,1:T(8,128)} %copy-done.4, f32[256,1,8,256]{3,0,2,1:T(8,128)} %copy-done.3, f32[256,1,8,256]{3,0,2,1:T(8,128)} %copy-done.2, f32[256,1,8,256]{3,0,2,1:T(8,128)} %copy-done.1, f32[256,1,8,256]{3,0,2,1:T(8,128)} %copy-done, ...), kind=kLoop, calls=%fused_computation.11 | loop fusion | flops 11534336 | bytes 16875520 | tf_op jit(solution)/shard_map/add | solution.py:29
  115.0 3.0 %copy.144 = f32[256,1,8,256]{0,3,2,1:T(8,128)} copy(f32[256,1,8,256]{3,0,2,1:T(8,128)} %get-tuple-element.22) | data formatting | bytes 4194304 | tf_op jit(solution)/shard_map/add | solution.py:29
  118.1 6.5 %multiply_add_fusion.5 = (f32[256,1,8,256]{3,0,2,1:T(8,128)}, f32[256,1,8,256]{3,0,2,1:T(8,128)}) fusion(f32[256,1,8,256]{3,0,2,1:T(8,128)} %copy-done.4, f32[256,1,8,256]{3,0,2,1:T(8,128)} %copy-done.3, f32[256,1,8,256]{3,0,2,1:T(8,128)} %copy-done.2, f32[256,1,8,256]{3,0,2,1:T(8,128)} %copy-done.1, f32[256,1,8,256]{3,0,2,1:T(8,128)} %copy-done, ...), kind=kLoop, calls=%fused_computation.13 | loop fusion | flops 11534336 | bytes 16875520 | tf_op jit(solution)/shard_map/add | solution.py:29
  124.7 3.0 %copy.138 = f32[256,1,8,256]{0,3,2,1:T(8,128)} copy(f32[256,1,8,256]{3,0,2,1:T(8,128)} %get-tuple-element.24) | data formatting | bytes 4194304 | tf_op jit(solution)/shard_map/add | solution.py:29
  127.8 6.5 %multiply_add_fusion.7 = (f32[256,1,8,256]{3,0,2,1:T(8,128)}, f32[256,1,8,256]{3,0,2,1:T(8,128)}) fusion(f32[256,1,8,256]{3,0,2,1:T(8,128)} %copy-done.4, f32[256,1,8,256]{3,0,2,1:T(8,128)} %copy-done.3, f32[256,1,8,256]{3,0,2,1:T(8,128)} %copy-done.2, f32[256,1,8,256]{3,0,2,1:T(8,128)} %copy-done.1, f32[256,1,8,256]{3,0,2,1:T(8,128)} %copy-done, ...), kind=kLoop, calls=%fused_computation.15 | loop fusion | flops 11534336 | bytes 16875520 | tf_op jit(solution)/shard_map/add | solution.py:29
  134.3 3.0 %copy.132 = f32[256,1,8,256]{0,3,2,1:T(8,128)} copy(f32[256,1,8,256]{3,0,2,1:T(8,128)} %get-tuple-element.26) | data formatting | bytes 4194304 | tf_op jit(solution)/shard_map/add | solution.py:29
  137.3 6.7 %multiply_add_fusion.9 = f32[256,1,8,256]{3,0,2,1:T(8,128)} fusion(f32[256,1,8,256]{3,0,2,1:T(8,128)} %copy-done.4, f32[256,1,8,256]{3,0,2,1:T(8,128)} %copy-done.3, f32[256,1,8,256]{3,0,2,1:T(8,128)} %copy-done.2, f32[256,1,8,256]{3,0,2,1:T(8,128)} %copy-done.1, f32[256,1,8,256]{3,0,2,1:T(8,128)} %copy-done, f32[256,1,8,256]{3,0,2,1:T(8,128)S(1)} %get-tuple-element.13, ...), kind=kLoop, calls=%fused_computation.17 | loop fusion | flops 5767168 | bytes 14729216 | tf_op jit(solution)/shard_map/add | solution.py:29
  147.5 2.9 %copy.135 = f32[256,1,8,256]{0,3,2,1:T(8,128)} copy(f32[256,1,8,256]{3,0,2,1:T(8,128)} %get-tuple-element.25) | data formatting | bytes 4194304 | tf_op jit(solution)/shard_map/add | solution.py:29
  150.4 3.0 %copy.141 = f32[256,1,8,256]{0,3,2,1:T(8,128)} copy(f32[256,1,8,256]{3,0,2,1:T(8,128)} %get-tuple-element.23) | data formatting | bytes 4194304 | tf_op jit(solution)/shard_map/add | solution.py:29
  155.3 3.0 %copy.153 = f32[256,1,8,256]{0,3,2,1:T(8,128)} copy(f32[256,1,8,256]{3,0,2,1:T(8,128)} %get-tuple-element.19) | data formatting | bytes 4194304 | tf_op jit(solution)/shard_map/add | solution.py:29
  160.1 3.2 %constant_dynamic-update-slice_fusion.8 = f32[10,256,2048]{1,2,0:T(8,128)} fusion(f32[10,256,2048]{1,2,0:T(8,128)} %constant_dynamic-update-slice_fusion.9, f32[1,256,2048]{1,2,0:T(8,128)} %bitcast.365), kind=kLoop, calls=%fused_computation.102 | loop fusion | bytes 4194304
  181.6 20.3 %broadcast_multiply_fusion = (f32[16,1,8,256]{3,0,2,1:T(8,128)S(1)}, f32[16,1,8,256]{3,0,2,1:T(8,128)S(1)}) fusion(f32[8,256,256,10]{2,1,0,3:T(8,128)} %bitcast.361, f32[10,256,256]{2,1,0:T(8,128)} %convert_reduce_fusion, s32[]{:T(128)S(6)} %select_n.3, f32[16,256]{1,0:T(8,128)S(1)} %copy-done.31, f32[10,256]{1,0:T(8,128)S(1)} %copy-done.30, ...), kind=kOutput, calls=%fused_computation.93 | convolution fusion | flops 1007575040 | bytes 22522500 | tf_op jit(solution)/shard_map/kij,kjc->ic/dot_general | solution.py:65
  202.0 4.3 %collective-permute-start.4 = (f32[16,1,8,256]{3,0,2,1:T(8,128)S(1)}, f32[16,1,8,256]{3,0,2,1:T(8,128)S(1)}, u32[]{:S(2)}, u32[]{:S(2)}) collective-permute-start(f32[16,1,8,256]{3,0,2,1:T(8,128)S(1)} %get-tuple-element.232), channel_id=1, source_target_pairs={{16,0},{32,16},{48,32},{64,48},{80,64},{96,80},{112,96},{128,112},... | collective-permute-start | bytes 393224 | tf_op jit(solution)/shard_map/ppermute | solution.py:17
  209.4 4.3 %collective-permute-done.5 = f32[16,1,8,256]{3,0,2,1:T(8,128)S(1)} collective-permute-done((f32[16,1,8,256]{3,0,2,1:T(8,128)S(1)}, f32[16,1,8,256]{3,0,2,1:T(8,128)S(1)}, u32[]{:S(2)}, u32[]{:S(2)}) %collective-permute-start.5) | collective-permute-done | bytes 131104 | tf_op jit(solution)/shard_map/ppermute | solution.py:16
  216.3 2.9 %collective-permute-done.6 = f32[16,1,8,256]{3,0,2,1:T(8,128)S(1)} collective-permute-done((f32[16,1,8,256]{3,0,2,1:T(8,128)S(1)}, f32[16,1,8,256]{3,0,2,1:T(8,128)S(1)}, u32[]{:S(2)}, u32[]{:S(2)}) %collective-permute-start.6) | collective-permute-done | bytes 131104 | tf_op jit(solution)/shard_map/ppermute | solution.py:17
  224.0 2.9 %collective-permute-done.8 = f32[16,1,8,256]{3,0,2,1:T(8,128)S(1)} collective-permute-done((f32[16,1,8,256]{3,0,2,1:T(8,128)S(1)}, f32[16,1,8,256]{3,0,2,1:T(8,128)S(1)}, u32[]{:S(2)}, u32[]{:S(2)}) %collective-permute-start.8) | collective-permute-done | bytes 131104 | tf_op jit(solution)/shard_map/ppermute | solution.py:17
  (293 shorter events, 63.0 us)
Async XLA Ops:
  7.2 79.9 %all-gather.2.cloned.1.call-start = ((), (), s32[]{:S(2)}) async-start(), calls=%async_computation | async-start | bytes 6684672 | tf_op jit(solution)/shard_map/all_gather | solution.py:61
  8.2 21.5 %copy-start.17 = (f32[1,8,256]{2,1,0:T(8,128)S(1)}, f32[1,8,256]{2,1,0:T(8,128)}, u32[]{:S(2)}) copy-start(f32[1,8,256]{2,1,0:T(8,128)} %param.8) | copy-start | bytes 24580
  8.2 21.4 %copy-start.16 = (f32[10,1,8,256]{3,2,1,0:T(8,128)S(1)}, f32[10,1,8,256]{3,2,1,0:T(8,128)}, u32[]{:S(2)}) copy-start(f32[10,1,8,256]{3,2,1,0:T(8,128)} %param.9) | copy-start | bytes 245764
  8.2 21.8 %copy-start.95 = (s32[256,10]{0,1:T(8,128)S(1)}, s32[256,10]{0,1:T(8,128)}, u32[]{:S(2)}) copy-start(s32[256,10]{0,1:T(8,128)} %param.11) | copy-start | bytes 30724
  8.2 8.7 %collective-permute-start.1 = (f32[16,1,8,256]{3,0,2,1:T(8,128)S(1)}, f32[16,1,8,256]{3,0,2,1:T(8,128)S(1)}, u32[]{:S(2)}, u32[]{:S(2)}) collective-permute-start(f32[16,1,8,256]{3,0,2,1:T(8,128)S(1)} %copy.125), channel_id=1, source_target_pairs={{16,0},{32,16},{48,32},{64,48},{80,64},{96,80},{112,96},{128,112},... | collective-permute-start | bytes 393224 | tf_op jit(solution)/shard_map/ppermute | solution.py:17
  14.1 7.1 %collective-permute-start.3 = (f32[16,1,8,256]{3,0,2,1:T(8,128)S(1)}, f32[16,1,8,256]{3,0,2,1:T(8,128)S(1)}, u32[]{:S(2)}, u32[]{:S(2)}) collective-permute-start(f32[16,1,8,256]{3,0,2,1:T(8,128)S(1)} %copy.125), channel_id=1, source_target_pairs={{0,16},{16,32},{32,48},{48,64},{64,80},{80,96},{96,112},{112,128},... | collective-permute-start | bytes 393224 | tf_op jit(solution)/shard_map/ppermute | solution.py:16
  22.9 11.2 %collective-permute-start = (f32[11,1,8,256]{3,2,1,0:T(8,128)S(1)}, f32[11,1,8,256]{3,2,1,0:T(8,128)S(1)}, u32[]{:S(2)}, u32[]{:S(2)}) collective-permute-start(f32[11,1,8,256]{3,2,1,0:T(8,128)S(1)} %pad_maximum_fusion.1), channel_id=1, source_target_pairs={{16,0},{32,16},{48,32},{64,48},{80,64},{96,80},{112,96},{128,112},... | collective-permute-start | bytes 270344 | tf_op jit(solution)/shard_map/ppermute | solution.py:17
  23.2 11.7 %collective-permute-start.2 = (f32[11,1,8,256]{3,2,1,0:T(8,128)S(1)}, f32[11,1,8,256]{3,2,1,0:T(8,128)S(1)}, u32[]{:S(2)}, u32[]{:S(2)}) collective-permute-start(f32[11,1,8,256]{3,2,1,0:T(8,128)S(1)} %pad_maximum_fusion.1), channel_id=1, source_target_pairs={{0,16},{16,32},{32,48},{48,64},{64,80},{80,96},{96,112},{112,128},... | collective-permute-start | bytes 270344 | tf_op jit(solution)/shard_map/ppermute | solution.py:16
  94.5 5.5 %copy-start.50 = (f32[8,256]{1,0:T(8,128)S(1)}, f32[8,256]{1,0:T(8,128)}, u32[]{:S(2)}) copy-start(f32[8,256]{1,0:T(8,128)} %get-tuple-element.104) | copy-start | bytes 24580
  94.5 5.5 %copy-start.51 = (f32[8,256]{1,0:T(8,128)S(1)}, f32[8,256]{1,0:T(8,128)}, u32[]{:S(2)}) copy-start(f32[8,256]{1,0:T(8,128)} %get-tuple-element.112) | copy-start | bytes 24580
  94.5 5.5 %copy-start.66 = (f32[8,256]{1,0:T(8,128)S(1)}, f32[8,256]{1,0:T(8,128)}, u32[]{:S(2)}) copy-start(f32[8,256]{1,0:T(8,128)} %get-tuple-element.114) | copy-start | bytes 24580
  94.5 5.5 %copy-start.69 = (f32[8,256]{1,0:T(8,128)S(1)}, f32[8,256]{1,0:T(8,128)}, u32[]{:S(2)}) copy-start(f32[8,256]{1,0:T(8,128)} %get-tuple-element.120) | copy-start | bytes 24580
  94.5 5.5 %copy-start.77 = (f32[8,256]{1,0:T(8,128)S(1)}, f32[8,256]{1,0:T(8,128)}, u32[]{:S(2)}) copy-start(f32[8,256]{1,0:T(8,128)} %get-tuple-element.91) | copy-start | bytes 24580
  94.5 5.5 %copy-start.78 = (f32[8,256]{1,0:T(8,128)S(1)}, f32[8,256]{1,0:T(8,128)}, u32[]{:S(2)}) copy-start(f32[8,256]{1,0:T(8,128)} %get-tuple-element.92) | copy-start | bytes 24580
  94.5 5.5 %copy-start.79 = (f32[8,256]{1,0:T(8,128)S(1)}, f32[8,256]{1,0:T(8,128)}, u32[]{:S(2)}) copy-start(f32[8,256]{1,0:T(8,128)} %get-tuple-element.93) | copy-start | bytes 24580
  94.5 5.5 %copy-start.80 = (f32[8,256]{1,0:T(8,128)S(1)}, f32[8,256]{1,0:T(8,128)}, u32[]{:S(2)}) copy-start(f32[8,256]{1,0:T(8,128)} %get-tuple-element.94) | copy-start | bytes 24580
  94.5 5.5 %copy-start.87 = (f32[8,256]{1,0:T(8,128)S(1)}, f32[8,256]{1,0:T(8,128)}, u32[]{:S(2)}) copy-start(f32[8,256]{1,0:T(8,128)} %get-tuple-element.35) | copy-start | bytes 24580
  94.5 5.5 %copy-start.88 = (f32[8,256]{1,0:T(8,128)S(1)}, f32[8,256]{1,0:T(8,128)}, u32[]{:S(2)}) copy-start(f32[8,256]{1,0:T(8,128)} %get-tuple-element.37) | copy-start | bytes 24580
  202.0 7.5 %collective-permute-start.4 = (f32[16,1,8,256]{3,0,2,1:T(8,128)S(1)}, f32[16,1,8,256]{3,0,2,1:T(8,128)S(1)}, u32[]{:S(2)}, u32[]{:S(2)}) collective-permute-start(f32[16,1,8,256]{3,0,2,1:T(8,128)S(1)} %get-tuple-element.232), channel_id=1, source_target_pairs={{16,0},{32,16},{48,32},{64,48},{80,64},{96,80},{112,96},{128,112},... | collective-permute-start | bytes 393224 | tf_op jit(solution)/shard_map/ppermute | solution.py:17
  206.3 7.5 %collective-permute-start.5 = (f32[16,1,8,256]{3,0,2,1:T(8,128)S(1)}, f32[16,1,8,256]{3,0,2,1:T(8,128)S(1)}, u32[]{:S(2)}, u32[]{:S(2)}) collective-permute-start(f32[16,1,8,256]{3,0,2,1:T(8,128)S(1)} %get-tuple-element.232), channel_id=1, source_target_pairs={{0,16},{16,32},{32,48},{48,64},{64,80},{80,96},{96,112},{112,128},... | collective-permute-start | bytes 393224 | tf_op jit(solution)/shard_map/ppermute | solution.py:16
  214.1 5.0 %collective-permute-start.6 = (f32[16,1,8,256]{3,0,2,1:T(8,128)S(1)}, f32[16,1,8,256]{3,0,2,1:T(8,128)S(1)}, u32[]{:S(2)}, u32[]{:S(2)}) collective-permute-start(f32[16,1,8,256]{3,0,2,1:T(8,128)S(1)} %get-tuple-element.10), channel_id=1, source_target_pairs={{16,0},{32,16},{48,32},{64,48},{80,64},{96,80},{112,96},{128,112},... | collective-permute-start | bytes 393224 | tf_op jit(solution)/shard_map/ppermute | solution.py:17
  214.4 7.1 %collective-permute-start.7 = (f32[16,1,8,256]{3,0,2,1:T(8,128)S(1)}, f32[16,1,8,256]{3,0,2,1:T(8,128)S(1)}, u32[]{:S(2)}, u32[]{:S(2)}) collective-permute-start(f32[16,1,8,256]{3,0,2,1:T(8,128)S(1)} %get-tuple-element.10), channel_id=1, source_target_pairs={{0,16},{16,32},{32,48},{48,64},{64,80},{80,96},{96,112},{112,128},... | collective-permute-start | bytes 393224 | tf_op jit(solution)/shard_map/ppermute | solution.py:16
  221.8 5.0 %collective-permute-start.8 = (f32[16,1,8,256]{3,0,2,1:T(8,128)S(1)}, f32[16,1,8,256]{3,0,2,1:T(8,128)S(1)}, u32[]{:S(2)}, u32[]{:S(2)}) collective-permute-start(f32[16,1,8,256]{3,0,2,1:T(8,128)S(1)} %get-tuple-element.8), channel_id=1, source_target_pairs={{16,0},{32,16},{48,32},{64,48},{80,64},{96,80},{112,96},{128,112},... | collective-permute-start | bytes 393224 | tf_op jit(solution)/shard_map/ppermute | solution.py:17
  221.9 7.2 %collective-permute-start.9 = (f32[16,1,8,256]{3,0,2,1:T(8,128)S(1)}, f32[16,1,8,256]{3,0,2,1:T(8,128)S(1)}, u32[]{:S(2)}, u32[]{:S(2)}) collective-permute-start(f32[16,1,8,256]{3,0,2,1:T(8,128)S(1)} %get-tuple-element.8), channel_id=1, source_target_pairs={{0,16},{16,32},{32,48},{48,64},{64,80},{80,96},{96,112},{112,128},... | collective-permute-start | bytes 393224 | tf_op jit(solution)/shard_map/ppermute | solution.py:16
  (83 other events, 230.0 us)
Sparse Core Ops, SparseCore 0:
  22.1 64.9 all-gather.1
where the time goes:
time: 238 us; the launch traced here: 237 us
  waiting for transfers between devices  69.2 us (29%)
  local copies, waits for them, and re-layouts  65.9 us (28%)
  other arithmetic  49.8 us (21%)
  matrix products  20.3 us (9%)
  starting transfers between devices  16.5 us (7%)
  between operations  15.2 us (6%)
    all_gather x1, waiting for transfers between devices, shards(): piece = lax.all_gather(padded_solution, 'ma', axis=0, tiled=True)  45.2 us
    add x6, other arithmetic, diffuse(): total + 0.5 * (center + jnp.roll(center, offset, which_dim)) * (values -...  36 us
    add x10, local copies, waits for them, and re-layouts, diffuse(): total + 0.5 * (center + jnp.roll(center, offset, which_dim)) * (values -...  26.6 us
    unnamed x204, local copies, waits for them, and re-layouts  24.9 us
    dot_general x1, matrix products, shards(): jnp.einsum('kij,kjc->ic', g_rows, terms, precision=lax.Precision.HIGHEST)  20.3 us
    ppermute x5, waiting for transfers between devices, extended(): before = lax.ppermute(last, axis, up)  13.2 us
    ppermute x5, starting transfers between devices, extended(): after = lax.ppermute(initial, axis, down)  10.9 us
    ppermute x5, waiting for transfers between devices, extended(): after = lax.ppermute(initial, axis, down)  10.8 us
  transfers between devices with their start and end apart: 11, of which 9 were waited for; matrix products, arithmetic and copies ran while one was open for 8% of the time, Pallas kernels for 0%

commit v1 on v0

v1 whole, which is shorter than its diff:
```python
import jax
import jax.numpy as jnp
from jax import lax
from jax.experimental import pallas as pl
from jax.experimental.pallas import tpu as pltpu
from jax.sharding import PartitionSpec as P

STEPS = 3
VMEM = pltpu.VMEM
SMEM = pltpu.SMEM


def ahead(a, axis):
    return pltpu.roll(a, a.shape[axis] - 1, axis)


def behind(a, axis):
    return pltpu.roll(a, 1, axis)


def mix_kernel(index, near_weight, far_weight, near, far, sol, src, mid, up, down, out, faces):
    fields = mid.shape[0]
    modes = sol.shape[0]
    for q in range(fields):
        center = mid[q]
        faces[q, 0] = 0.5 * (center + up[q])
        faces[q, 1] = 0.5 * (center + down[q])
        for d, axis in ((2, 0), (4, 1)):
            face = 0.5 * (center + ahead(center, axis))
            faces[q, d] = face
            faces[q, d + 1] = behind(face, axis)

    @pl.loop(0, modes)
    def _(i):
        value = sol[i]
        sums = [faces[0, d] * value for d in range(6)]
        for k in range(fields - 1):
            mixed = None
            for s in range(2):
                at = (k * modes + i) * 2 + s
                j = index[at]
                term = near_weight[at] * near[j] + far_weight[at] * far[j]
                mixed = term if mixed is None else mixed + term
            sums = [sums[d] + faces[k + 1, d] * mixed for d in range(6)]
        image = value
        for d, axis in ((2, 0), (4, 1)):
            flux = sums[d] - ahead(sums[d + 1], axis)
            image = image + (flux - behind(flux, axis))
        out[i, 0] = src[i] - image
        out[i, 1] = sums[0]
        out[i, 2] = sums[1]
        out[i, 3] = mid[0]


def cheb_kernel(got, out, faces, direction, remain):
    planes = got.shape[0]
    for x in range(planes):
        center = got[x, 3]
        faces[x, 0] = 0.5 * (center + got[(x + 1) % planes, 3])
        faces[x, 1] = 0.5 * (center + ahead(center, 0))
        faces[x, 2] = 0.5 * (center + ahead(center, 1))
    theta = 13.0
    delta = 12.0
    sigma = theta / delta
    rho = 1.0 / sigma
    for x in range(planes):
        before, after = (x - 1) % planes, (x + 1) % planes
        image = (got[x, 1] - got[after, 2]) + (got[x, 2] - got[before, 1])
        residual = got[x, 0] - image
        first = residual * (1.0 / theta)
        out[x, 0] = residual
        out[x, 1] = first
        remain[x] = residual
        direction[0, x] = first
    for step in range(STEPS):
        now, later = step % 2, (step + 1) % 2
        rho_next = 1.0 / (2.0 * sigma - rho)
        flux_x = faces[planes - 1, 0] * (direction[now, planes - 1] - direction[now, 0])
        for x in range(planes):
            value = direction[now, x]
            flux_next = faces[x, 0] * (value - direction[now, (x + 1) % planes])
            applied = value + (flux_next - flux_x)
            flux_x = flux_next
            for axis in (0, 1):
                flux = faces[x, axis + 1] * (value - ahead(value, axis))
                applied = applied + (flux - behind(flux, axis))
            left = remain[x] - applied
            remain[x] = left
            new = (rho_next * rho) * value + (2.0 * rho_next / delta) * left
            direction[later, x] = new
            out[x, 1] = out[x, 1] + new
        rho = rho_next


def whole(memory):
    return pl.BlockSpec(memory_space=memory)


def shards(solution, source, mean_conductivity, kl_fields, couplings, mode_index):
    modes, _, ny, nz = solution.shape
    planes = lax.axis_size("gx")
    blocks = lax.axis_size("ma")
    chips = blocks // 2
    block = lax.axis_index("ma")
    core = block % 2
    sol = solution[:, 0]
    src = source[:, 0]
    mid = jnp.concatenate([mean_conductivity, kl_fields[:, 0]], 0)
    fields = mid.shape[0]

    ring = [(i, (i + 1) % planes) for i in range(planes)]
    down = lax.ppermute(mid, "gx", ring)
    up = lax.ppermute(mid, "gx", [(j, i) for i, j in ring])

    same_core = [[2 * chip + c for chip in range(chips)] for c in range(2)]
    spread = jnp.broadcast_to(sol[None], (chips,) + sol.shape)
    near = lax.all_to_all(spread, "ma", 0, 0, tiled=True, axis_index_groups=same_core)
    far = lax.ppermute(near, "ma", [(i, i ^ 1) for i in range(blocks)])

    rows = lax.dynamic_slice_in_dim(couplings, block * modes, modes, 1)
    own = block * modes + lax.broadcasted_iota(jnp.int32, rows.shape, 1)
    degree = lax.dynamic_slice_in_dim(mode_index, block * modes, modes, 0).T
    higher = degree[:, :, None] + (1 - lax.broadcasted_iota(jnp.int32, rows.shape, 2))
    weight = jnp.where(rows != own, jnp.sqrt(higher.astype(jnp.float32)), 0.0)
    owner = rows // modes
    is_near = (owner % 2) == core
    index = ((owner // 2) * modes + rows % modes).reshape(-1)
    near_weight = jnp.where(is_near, weight, 0.0).reshape(-1)
    far_weight = jnp.where(is_near, 0.0, weight).reshape(-1)

    tile = (ny, nz)
    mixed = pl.pallas_call(
        mix_kernel,
        out_shape=jax.ShapeDtypeStruct((modes, 4) + tile, jnp.float32),
        in_specs=[whole(SMEM)] * 3 + [whole(VMEM)] * 7,
        out_specs=whole(VMEM),
        scratch_shapes=[VMEM((fields, 6) + tile, jnp.float32)],
        name="mix",
    )(
        index, near_weight, far_weight,
        near.reshape((chips * modes,) + tile), far.reshape((chips * modes,) + tile),
        sol, src, mid, up, down,
    )
    got = lax.all_to_all(mixed, "gx", 0, 0, tiled=True)
    done = pl.pallas_call(
        cheb_kernel,
        out_shape=jax.ShapeDtypeStruct((planes, 2) + tile, jnp.float32),
        in_specs=[whole(VMEM)],
        out_specs=whole(VMEM),
        scratch_shapes=[
            VMEM((planes, 3) + tile, jnp.float32),
            VMEM((2, planes) + tile, jnp.float32),
            VMEM((planes,) + tile, jnp.float32),
        ],
        name="cheb",
    )(got)
    back = lax.all_to_all(done, "gx", 0, 0, tiled=True)
    return (back[:, 0:1], back[:, 1:2])


def solution(mesh):
    in_specs = (
        P("ma", "gx", None, None),
        P("ma", "gx", None, None),
        P("gx", None, None),
        P(None, "gx", None, None),
        P(),
        P(),
    )
    out_specs = (P("ma", "gx", None, None), P("ma", "gx", None, None))
    return jax.shard_map(shards, mesh=mesh, in_specs=in_specs, out_specs=out_specs, check_vma=False)
```

time: 238 us -> 81.8 us (0.34)
  waiting for transfers between devices: 69.2 us -> 0.01 us
  local copies, waits for them, and re-layouts: 65.9 us -> 6 us
  blocking collectives: 0 us -> 59.3 us
  other arithmetic: 49.8 us -> 0.25 us
  matrix products: 20.3 us -> 0 us
  between operations: 15.2 us -> 0.76 us
  starting transfers between devices: 16.5 us -> 6.81 us
  Pallas kernels: 0 us -> 7.95 us
    all_to_all x0 -> x3, blocking collectives: none -> 59.3 us  [the longest x1 23.3 us: shards(): lax.all_to_all(spread, 'ma', 0, 0, tiled=True, axis_index_groups=same_core)]
    all_gather x1 -> x0, waiting for transfers between devices: 45.2 us -> none  [shards(): piece = lax.all_gather(padded_solution, 'ma', axis=0, tiled=True)]
    add x9 -> x2, other arithmetic: 36.6 us -> 0.1 us  [the longest x1 0.1 us: shards(): index = (owner // 2 * modes + rows % modes).reshape(-1)]
    add x10 -> x1, local copies, waits for them, and re-layouts: 26.6 us -> 0.13 us  [shards(): index = (owner // 2 * modes + rows % modes).reshape(-1)]
    ppermute x10 -> x3, waiting for transfers between devices: 24 us -> 0.01 us  [the longest x1 0.01 us: shards(): down = lax.ppermute(mid, 'gx', ring)]
    unnamed x204 -> x18, local copies, waits for them, and re-layouts: 24.9 us -> 1.69 us
    dot_general x1 -> x0, matrix products: 20.3 us -> none  [shards(): jnp.einsum('kij,kjc->ic', g_rows, terms, precision=lax.Precision.HIGHEST)]
    slice x21 -> x1, local copies, waits for them, and re-layouts: 10.4 us -> 0.72 us  [shards(): return (back[:, 0:1], back[:, 1:2])]
  transfers between devices with their start and end apart: 11 -> 3, of which waited for: 9 -> 0; matrix products, arithmetic and copies ran while one was open for 8% -> 4% of each run, Pallas kernels for 0% -> 0%
where the time goes in v1:
time: 81.8 us; the launch traced here: 81.1 us
  blocking collectives  59.3 us (72%)
  Pallas kernels  7.95 us (10%)
  starting transfers between devices  6.81 us (8%)
  local copies, waits for them, and re-layouts  6 us (7%)
    all_to_all x1, blocking collectives, shards(): lax.all_to_all(spread, 'ma', 0, 0, tiled=True, axis_index_groups=same_core)  23.3 us
    all_to_all x1, blocking collectives, shards(): got = lax.all_to_all(mixed, 'gx', 0, 0, tiled=True)  21.2 us
    all_to_all x1, blocking collectives, shards(): back = lax.all_to_all(done, 'gx', 0, 0, tiled=True)  14.9 us
    pallas_call x1, Pallas kernels, shards(): pl.pallas_call(mix_kernel, out_shape=jax.ShapeDtypeStruct((modes, 4) + ti...  5.67 us
    ppermute x1, starting transfers between devices, shards(): up = lax.ppermute(mid, 'gx', [(j, i) for i, j in ring])  4.81 us
    pallas_call x1, Pallas kernels, shards(): pl.pallas_call(cheb_kernel, out_shape=jax.ShapeDtypeStruct((planes, 2) +...  2.28 us
    ppermute x1, starting transfers between devices, shards(): down = lax.ppermute(mid, 'gx', ring)  1.99 us
    unnamed x18, local copies, waits for them, and re-layouts  1.69 us
  transfers between devices with their start and end apart: 3, of which 0 were waited for; matrix products, arithmetic and copies ran while one was open for 4% of the time, Pallas kernels for 0%

profile of v1, /device:TPU:2, one launch (start us, length us, event | category | flops | bytes accessed | tf_op | source)
XLA Modules:
  0.0 81.1 jit_solution(2948582523945377491)
XLA Ops:
  0.6 0.0 copy-start
  0.6 1.0 %broadcast_in_dim.17 = f32[8,16,8,256]{3,2,1,0:T(8,128)S(1)} broadcast(f32[16,8,256]{2,1,0:T(8,128)} %bitcast.9), dimensions={1,2,3} | broadcast | bytes 1179648 | tf_op jit(solution)/shard_map/broadcast_in_dim | solution.py:116
  1.7 0.0 copy-start.8
  1.7 23.3 %all_to_all.15 = f32[8,16,8,256]{3,2,1,0:T(8,128)S(1)} all-to-all(f32[8,16,8,256]{3,2,1,0:T(8,128)S(1)} %broadcast_in_dim.17), channel_id=1, replica_groups={{0,2,4,6,8,10,12,14},{1,3,5,7,9,11,13,15},{16,18,20,22,24,26,28,30},{17..., dimensions={0} | all-to-all | bytes 2097152 | tf_op jit(solution)/shard_map/all_to_all | solution.py:117
  25.0 2.0 %collective-permute-start.2 = (f32[11,8,256]{2,1,0:T(8,128)S(1)}, f32[11,8,256]{2,1,0:T(8,128)S(1)}, u32[]{:S(2)}, u32[]{:S(2)}) collective-permute-start(f32[11,8,256]{2,1,0:T(8,128)S(1)} %pad_maximum_fusion.mid), channel_id=1, source_target_pairs={{0,16},{16,32},{32,48},{48,64},{64,80},{80,96},{96,112},{112,128},... | collective-permute-start | bytes 270344 | tf_op jit(solution)/shard_map/ppermute | solution.py:112
  27.0 4.8 %collective-permute-start.1 = (f32[11,8,256]{2,1,0:T(8,128)S(1)}, f32[11,8,256]{2,1,0:T(8,128)S(1)}, u32[]{:S(2)}, u32[]{:S(2)}) collective-permute-start(f32[11,8,256]{2,1,0:T(8,128)S(1)} %pad_maximum_fusion.mid), channel_id=1, source_target_pairs={{16,0},{32,16},{48,32},{64,48},{80,64},{96,80},{112,96},{128,112},... | collective-permute-start | bytes 270344 | tf_op jit(solution)/shard_map/ppermute | solution.py:113
  31.8 0.1 dynamic-slice_bitcast_fusion
  31.9 0.6 copy-done.7
  32.5 0.1 broadcast_select_fusion
  32.7 0.1 fusion
  32.8 0.1 copy.9
  32.9 0.7 reshape.22.near_weight
  33.6 0.1 copy.8
  33.7 0.7 reshape.21.index
  34.4 0.1 copy.10
  34.6 0.7 reshape.23.far_weight
  35.3 0.6 copy-done.4
  35.9 0.0 copy-done.5
  36.0 0.4 copy-done.2
  36.4 5.7 %mix.1 = f32[16,4,8,256]{3,2,1,0:T(8,128)} custom-call(s32[320]{0:T(512)} %reshape.21.index, f32[320]{0:T(512)} %reshape.22.near_weight, f32[320]{0:T(512)} %reshape.23.far_weight, f32[128,8,256]{2,1,0:T(8,128)} %bitcast.7, f32[128,8,256]{2,1,0:T(8,128)} %bitcast.8, f32[16,8,256]{2,1,0:T(8,128)} %bitcast.10, f32[16,8,256]{2,1,0:T(8,128)} %bitcast.11, ...), custom_call_target="tpu_custom_call" | custom-call | tf_op jit(solution)/shard_map/mix/pallas_call | solution.py:132
  42.0 21.2 %all_to_all.16.got = f32[16,4,8,256]{3,2,1,0:T(8,128)} all-to-all(f32[16,4,8,256]{3,2,1,0:T(8,128)} %mix.1), channel_id=1, replica_groups=mesh['gx'=16,'ma'=16] {'gx'}, dimensions={0} | all-to-all | bytes 1048576 | tf_op jit(solution)/shard_map/all_to_all | solution.py:144
  63.2 2.3 %cheb.1 = f32[16,2,8,256]{3,2,1,0:T(8,128)} custom-call(f32[16,4,8,256]{3,2,1,0:T(8,128)} %all_to_all.16.got), custom_call_target="tpu_custom_call" | custom-call | tf_op jit(solution)/shard_map/cheb/pallas_call | solution.py:145
  65.5 14.9 %all_to_all.17 = f32[16,2,8,256]{3,2,1,0:T(8,128)S(1)} all-to-all(f32[16,2,8,256]{3,2,1,0:T(8,128)} %cheb.1), channel_id=1, replica_groups=mesh['gx'=16,'ma'=16] {'gx'}, dimensions={0} | all-to-all | bytes 524288 | tf_op jit(solution)/shard_map/all_to_all | solution.py:157
  80.3 0.7 fusion.3
  (20 shorter events, 0.1 us)
Async XLA Ops:
  0.6 31.2 %copy-start = (s32[256,10]{0,1:T(8,128)S(1)}, s32[256,10]{0,1:T(8,128)}, u32[]{:S(2)}) copy-start(s32[256,10]{0,1:T(8,128)} %param.11) | copy-start | bytes 30724
  1.6 23.3 %copy-start.6 = (f32[10,1,8,256]{3,2,1,0:T(8,128)S(1)}, f32[10,1,8,256]{3,2,1,0:T(8,128)}, u32[]{:S(2)}) copy-start(f32[10,1,8,256]{3,2,1,0:T(8,128)} %param.9) | copy-start | bytes 245764
  1.7 23.3 %copy-start.8 = (f32[1,8,256]{2,1,0:T(8,128)S(1)}, f32[1,8,256]{2,1,0:T(8,128)}, u32[]{:S(2)}) copy-start(f32[1,8,256]{2,1,0:T(8,128)} %param.8) | copy-start | bytes 24580
  24.9 10.4 %copy-start.1 = (f32[8,16,8,256]{3,2,1,0:T(8,128)}, f32[8,16,8,256]{3,2,1,0:T(8,128)S(1)}, u32[]{:S(2)}) copy-start(f32[8,16,8,256]{3,2,1,0:T(8,128)S(1)} %all_to_all.15) | copy-start | bytes 3145732
  24.9 10.4 %collective-permute-start = (f32[8,16,8,256]{3,2,1,0:T(8,128)S(1)}, f32[8,16,8,256]{3,2,1,0:T(8,128)S(1)}, u32[]{:S(2)}, u32[]{:S(2)}) collective-permute-start(f32[8,16,8,256]{3,2,1,0:T(8,128)S(1)} %all_to_all.15), channel_id=1, source_target_pairs={{0,1},{1,0},{2,3},{3,2},{4,5},{5,4},{6,7},{7,6},{8,9},{9,8},{10,11... | collective-permute-start | bytes 3145736 | tf_op jit(solution)/shard_map/ppermute | solution.py:118
  25.0 7.9 %copy-start.3 = (f32[11,8,256]{2,1,0:T(8,128)}, f32[11,8,256]{2,1,0:T(8,128)S(1)}, u32[]{:S(2)}) copy-start(f32[11,8,256]{2,1,0:T(8,128)S(1)} %pad_maximum_fusion.mid) | copy-start | bytes 270340
  25.0 10.3 %collective-permute-start.2 = (f32[11,8,256]{2,1,0:T(8,128)S(1)}, f32[11,8,256]{2,1,0:T(8,128)S(1)}, u32[]{:S(2)}, u32[]{:S(2)}) collective-permute-start(f32[11,8,256]{2,1,0:T(8,128)S(1)} %pad_maximum_fusion.mid), channel_id=1, source_target_pairs={{0,16},{16,32},{32,48},{48,64},{64,80},{80,96},{96,112},{112,128},... | collective-permute-start | bytes 270344 | tf_op jit(solution)/shard_map/ppermute | solution.py:112
  27.0 8.3 %collective-permute-start.1 = (f32[11,8,256]{2,1,0:T(8,128)S(1)}, f32[11,8,256]{2,1,0:T(8,128)S(1)}, u32[]{:S(2)}, u32[]{:S(2)}) collective-permute-start(f32[11,8,256]{2,1,0:T(8,128)S(1)} %pad_maximum_fusion.mid), channel_id=1, source_target_pairs={{16,0},{32,16},{48,32},{64,48},{80,64},{96,80},{112,96},{128,112},... | collective-permute-start | bytes 270344 | tf_op jit(solution)/shard_map/ppermute | solution.py:113
  31.8 0.7 copy-start.7
  35.3 0.6 copy-start.4
  35.3 0.7 copy-start.5
  35.3 1.0 %copy-start.2 = (f32[8,16,8,256]{3,2,1,0:T(8,128)}, f32[8,16,8,256]{3,2,1,0:T(8,128)S(1)}, u32[]{:S(2)}) copy-start(f32[8,16,8,256]{3,2,1,0:T(8,128)S(1)} %collective-permute-done) | copy-start | bytes 3145732

commit v2 on v1

--- a/solution.py
+++ b/solution.py
@@ -18,9 +18,17 @@
     return pltpu.roll(a, 1, axis)
 
 
-def mix_kernel(index, near_weight, far_weight, near, far, sol, src, mid, up, down, out, faces):
+def mixture(index, weight, modes_in, k, i):
+    mixed = None
+    for s in range(2):
+        at = 2 * k + s
+        term = weight[at, i] * modes_in[index[at, i]]
+        mixed = term if mixed is None else mixed + term
+    return mixed
+
+
+def near_kernel(index, weight, near, sol, mid, up, down, sums, faces):
     fields = mid.shape[0]
-    modes = sol.shape[0]
     for q in range(fields):
         center = mid[q]
         faces[q, 0] = 0.5 * (center + up[q])
@@ -30,25 +38,31 @@
             faces[q, d] = face
             faces[q, d + 1] = behind(face, axis)
 
-    @pl.loop(0, modes)
+    @pl.loop(0, sol.shape[0])
     def _(i):
         value = sol[i]
-        sums = [faces[0, d] * value for d in range(6)]
+        parts = [faces[0, d] * value for d in range(6)]
         for k in range(fields - 1):
-            mixed = None
-            for s in range(2):
-                at = (k * modes + i) * 2 + s
-                j = index[at]
-                term = near_weight[at] * near[j] + far_weight[at] * far[j]
-                mixed = term if mixed is None else mixed + term
-            sums = [sums[d] + faces[k + 1, d] * mixed for d in range(6)]
-        image = value
+            mixed = mixture(index, weight, near, k, i)
+            parts = [parts[d] + faces[k + 1, d] * mixed for d in range(6)]
+        for d in range(6):
+            sums[i, d] = parts[d]
+
+
+def far_kernel(index, weight, far, sol, src, mid, sums, faces, out):
+    @pl.loop(0, sol.shape[0])
+    def _(i):
+        parts = [sums[i, d] for d in range(6)]
+        for k in range(faces.shape[0] - 1):
+            mixed = mixture(index, weight, far, k, i)
+            parts = [parts[d] + faces[k + 1, d] * mixed for d in range(6)]
+        image = sol[i]
         for d, axis in ((2, 0), (4, 1)):
-            flux = sums[d] - ahead(sums[d + 1], axis)
+            flux = parts[d] - ahead(parts[d + 1], axis)
             image = image + (flux - behind(flux, axis))
         out[i, 0] = src[i] - image
-        out[i, 1] = sums[0]
-        out[i, 2] = sums[1]
+        out[i, 1] = parts[0]
+        out[i, 2] = parts[1]
         out[i, 3] = mid[0]
 
 
@@ -96,7 +110,23 @@
     return pl.BlockSpec(memory_space=memory)
 
 
-def shards(solution, source, mean_conductivity, kl_fields, couplings, mode_index):
+def kernel_of(body, outs, memories, scratch=(), flops=0, size=0):
+    return pl.pallas_call(
+        body,
+        out_shape=outs,
+        in_specs=[whole(m) for m in memories],
+        out_specs=jax.tree.map(lambda _: whole(VMEM), outs),
+        scratch_shapes=list(scratch),
+        compiler_params=pltpu.CompilerParams(vmem_limit_bytes=8 << 20),
+        cost_estimate=pl.CostEstimate(flops=flops, bytes_accessed=size, transcendentals=0),
+    )
+
+
+def f32(*shape):
+    return jax.ShapeDtypeStruct(shape, jnp.float32)
+
+
+def step(solution, source, mean_conductivity, kl_fields, couplings, mode_index):
     modes, _, ny, nz = solution.shape
     planes = lax.axis_size("gx")
     blocks = lax.axis_size("ma")
@@ -117,42 +147,34 @@
     near = lax.all_to_all(spread, "ma", 0, 0, tiled=True, axis_index_groups=same_core)
     far = lax.ppermute(near, "ma", [(i, i ^ 1) for i in range(blocks)])
 
-    rows = lax.dynamic_slice_in_dim(couplings, block * modes, modes, 1)
-    own = block * modes + lax.broadcasted_iota(jnp.int32, rows.shape, 1)
+    rows = lax.dynamic_slice_in_dim(couplings, block * modes, modes, 1).transpose(0, 2, 1)
+    own = block * modes + lax.broadcasted_iota(jnp.int32, rows.shape, 2)
     degree = lax.dynamic_slice_in_dim(mode_index, block * modes, modes, 0).T
-    higher = degree[:, :, None] + (1 - lax.broadcasted_iota(jnp.int32, rows.shape, 2))
+    higher = degree[:, None, :] + (1 - lax.broadcasted_iota(jnp.int32, rows.shape, 1))
     weight = jnp.where(rows != own, jnp.sqrt(higher.astype(jnp.float32)), 0.0)
-    owner = rows // modes
-    is_near = (owner % 2) == core
-    index = ((owner // 2) * modes + rows % modes).reshape(-1)
-    near_weight = jnp.where(is_near, weight, 0.0).reshape(-1)
-    far_weight = jnp.where(is_near, 0.0, weight).reshape(-1)
+    owner = rows >> (modes.bit_length() - 1)
+    is_near = (owner & 1) == core
+    flat = (2 * (fields - 1), modes)
+    index = ((owner >> 1) * modes + (rows & (modes - 1))).reshape(flat)
+    near_weight = jnp.where(is_near, weight, 0.0).reshape(flat)
+    far_weight = jnp.where(is_near, 0.0, weight).reshape(flat)
 
     tile = (ny, nz)
-    mixed = pl.pallas_call(
-        mix_kernel,
-        out_shape=jax.ShapeDtypeStruct((modes, 4) + tile, jnp.float32),
-        in_specs=[whole(SMEM)] * 3 + [whole(VMEM)] * 7,
-        out_specs=whole(VMEM),
-        scratch_shapes=[VMEM((fields, 6) + tile, jnp.float32)],
-        name="mix",
-    )(
-        index, near_weight, far_weight,
-        near.reshape((chips * modes,) + tile), far.reshape((chips * modes,) + tile),
-        sol, src, mid, up, down,
-    )
+    cell = ny * nz
+    pool = (chips * modes,) + tile
+    sums, faces = kernel_of(
+        near_kernel, (f32(modes, 6, *tile), f32(fields, 6, *tile)), [SMEM] * 2 + [VMEM] * 5,
+        flops=modes * fields * 16 * cell, size=4 * cell * (chips * modes + 8 * modes + 9 * fields),
+    )(index, near_weight, near.reshape(pool), sol, mid, up, down)
+    mixed = kernel_of(
+        far_kernel, f32(modes, 4, *tile), [SMEM] * 2 + [VMEM] * 6,
+        flops=modes * fields * 16 * cell, size=4 * cell * (chips * modes + 12 * modes + 7 * fields),
+    )(index, far_weight, far.reshape(pool), sol, src, mid, sums, faces)
     got = lax.all_to_all(mixed, "gx", 0, 0, tiled=True)
-    done = pl.pallas_call(
-        cheb_kernel,
-        out_shape=jax.ShapeDtypeStruct((planes, 2) + tile, jnp.float32),
-        in_specs=[whole(VMEM)],
-        out_specs=whole(VMEM),
-        scratch_shapes=[
-            VMEM((planes, 3) + tile, jnp.float32),
-            VMEM((2, planes) + tile, jnp.float32),
-            VMEM((planes,) + tile, jnp.float32),
-        ],
-        name="cheb",
+    done = kernel_of(
+        cheb_kernel, f32(planes, 2, *tile), [VMEM],
+        [VMEM((planes, 3) + tile, jnp.float32), VMEM((2, planes) + tile, jnp.float32), VMEM((planes,) + tile, jnp.float32)],
+        flops=planes * STEPS * 30 * cell, size=4 * cell * planes * 6,
     )(got)
     back = lax.all_to_all(done, "gx", 0, 0, tiled=True)
     return (back[:, 0:1], back[:, 1:2])
@@ -168,4 +190,4 @@
         P(),
     )
     out_specs = (P("ma", "gx", None, None), P("ma", "gx", None, None))
-    return jax.shard_map(shards, mesh=mesh, in_specs=in_specs, out_specs=out_specs, check_vma=False)
+    return jax.shard_map(step, mesh=mesh, in_specs=in_specs, out_specs=out_specs, check_vma=False)

time: 81.8 us -> 78.4 us (0.958)
  waiting for transfers between devices: 0.01 us -> 6.4 us
  local copies, waits for them, and re-layouts: 6 us -> 1.86 us
  blocking collectives: 59.3 us -> 55.4 us
  Pallas kernels: 7.95 us -> 6.45 us
    ppermute x3, waiting for transfers between devices: 0.01 us -> 6.4 us  [the longest x1 4.31 us: step(): down = lax.ppermute(mid, 'gx', ring)]
    all_to_all x3, blocking collectives: 59.3 us -> 55.4 us  [the longest x1 23.3 us: step(): lax.all_to_all(spread, 'ma', 0, 0, tiled=True, axis_index_groups=same_core)]
    reshape x3, local copies, waits for them, and re-layouts: 2.12 us -> 0.03 us  [the longest x1 0.01 us: step(): near_weight = jnp.where(is_near, weight, 0.0).reshape(flat)]
    unnamed x18 -> x12, local copies, waits for them, and re-layouts: 1.69 us -> 0.04 us
    pallas_call x2 -> x3, Pallas kernels: 7.95 us -> 6.45 us  [the longest x1 3.87 us: step(): kernel_of(far_kernel, f32(modes, 4, *tile), [SMEM] * 2 + [VMEM] * 6, flop...]
  transfers between devices with their start and end apart: 3 -> 3, of which waited for: 0 -> 2; matrix products, arithmetic and copies ran while one was open for 4% -> 1% of each run, Pallas kernels for 0% -> 3%
where the time goes in v2:
time: 78.4 us; the launch traced here: 77.9 us
  blocking collectives  55.4 us (71%)
  starting transfers between devices  6.72 us (9%)
  Pallas kernels  6.45 us (8%)
  waiting for transfers between devices  6.4 us (8%)
  local copies, waits for them, and re-layouts  1.86 us (2%)
    all_to_all x1, blocking collectives, step(): lax.all_to_all(spread, 'ma', 0, 0, tiled=True, axis_index_groups=same_core)  23.3 us
    all_to_all x1, blocking collectives, step(): got = lax.all_to_all(mixed, 'gx', 0, 0, tiled=True)  17.4 us
    all_to_all x1, blocking collectives, step(): back = lax.all_to_all(done, 'gx', 0, 0, tiled=True)  14.8 us
    ppermute x1, starting transfers between devices, step(): up = lax.ppermute(mid, 'gx', [(j, i) for i, j in ring])  6.71 us
    ppermute x1, waiting for transfers between devices, step(): down = lax.ppermute(mid, 'gx', ring)  4.31 us
    pallas_call x1, Pallas kernels, step(): kernel_of(far_kernel, f32(modes, 4, *tile), [SMEM] * 2 + [VMEM] * 6, flop...  3.87 us
    ppermute x1, waiting for transfers between devices, step(): up = lax.ppermute(mid, 'gx', [(j, i) for i, j in ring])  2.09 us
    pallas_call x1, Pallas kernels, step(): kernel_of(near_kernel, (f32(modes, 6, *tile), f32(fields, 6, *tile)), [SM...  2.05 us
  transfers between devices with their start and end apart: 3, of which 2 were waited for; matrix products, arithmetic and copies ran while one was open for 1% of the time, Pallas kernels for 3%

profile of v2, /device:TPU:2, one launch (start us, length us, event | category | flops | bytes accessed | tf_op | source)
XLA Modules:
  0.0 77.9 jit_solution(11906551744141341282)
XLA Ops:
  0.6 0.0 copy-start
  0.6 1.0 %broadcast_in_dim.17 = f32[8,16,8,256]{3,2,1,0:T(8,128)S(1)} broadcast(f32[16,8,256]{2,1,0:T(8,128)} %bitcast.16), dimensions={1,2,3} | broadcast | bytes 1179648 | tf_op jit(solution)/shard_map/broadcast_in_dim | solution.py:146
  1.6 0.0 copy-start.3
  1.7 0.0 copy-start.5
  1.7 23.3 %all_to_all.15 = f32[8,16,8,256]{3,2,1,0:T(8,128)S(1)} all-to-all(f32[8,16,8,256]{3,2,1,0:T(8,128)S(1)} %broadcast_in_dim.17), channel_id=1, replica_groups={{0,2,4,6,8,10,12,14},{1,3,5,7,9,11,13,15},{16,18,20,22,24,26,28,30},{17..., dimensions={0} | all-to-all | bytes 2097152 | tf_op jit(solution)/shard_map/all_to_all | solution.py:147
  24.9 0.0 collective-permute-start
  24.9 0.0 copy-start.4
  25.0 0.0 copy-start.1
  25.0 6.7 %collective-permute-start.1 = (f32[11,8,256]{2,1,0:T(8,128)S(1)}, f32[11,8,256]{2,1,0:T(8,128)S(1)}, u32[]{:S(2)}, u32[]{:S(2)}) collective-permute-start(f32[11,8,256]{2,1,0:T(8,128)S(1)} %pad_maximum_fusion.mid), channel_id=1, source_target_pairs={{16,0},{32,16},{48,32},{64,48},{80,64},{96,80},{112,96},{128,112},... | collective-permute-start | bytes 270344 | tf_op jit(solution)/shard_map/ppermute | solution.py:143
  31.7 0.0 collective-permute-start.2
  31.7 0.1 dynamic-slice_bitcast_fusion
  31.8 0.1 bitcast_select_fusion.1
  31.9 0.1 bitcast_select_fusion.2
  32.0 0.1 add_bitcast_fusion
  32.1 2.1 %collective-permute-done.1.up = f32[11,8,256]{2,1,0:T(8,128)S(1)} collective-permute-done((f32[11,8,256]{2,1,0:T(8,128)S(1)}, f32[11,8,256]{2,1,0:T(8,128)S(1)}, u32[]{:S(2)}, u32[]{:S(2)}) %collective-permute-start.1) | collective-permute-done | bytes 90144 | tf_op jit(solution)/shard_map/ppermute | solution.py:143
  34.2 4.3 %collective-permute-done.2.down = f32[11,8,256]{2,1,0:T(8,128)S(1)} collective-permute-done((f32[11,8,256]{2,1,0:T(8,128)S(1)}, f32[11,8,256]{2,1,0:T(8,128)S(1)}, u32[]{:S(2)}, u32[]{:S(2)}) %collective-permute-start.2) | collective-permute-done | bytes 90144 | tf_op jit(solution)/shard_map/ppermute | solution.py:142
  38.5 0.0 copy-done.1
  38.5 2.1 %shard_map.77 = (f32[16,6,8,256]{3,2,1,0:T(8,128)S(1)}, f32[11,6,8,256]{3,2,1,0:T(8,128)S(1)}) custom-call(s32[20,16]{1,0:T(8,128)S(1)} %reshape.21.index, f32[20,16]{1,0:T(8,128)S(1)} %reshape.24.weight, f32[128,8,256]{2,1,0:T(8,128)S(1)} %bitcast.15, f32[16,8,256]{2,1,0:T(8,128)S(1)} %bitcast.17, f32[11,8,256]{2,1,0:T(8,128)S(1)} %pad_maximum_fusion.mid, ...), custom_call_target="tpu_custom_call" | custom-call | flops 5767168 | bytes 2908160 | tf_op jit(solution)/shard_map/pallas_call | solution.py:165
  40.6 0.0 collective-permute-done
  40.6 3.9 %shard_map.78 = f32[16,4,8,256]{3,2,1,0:T(8,128)S(1)} custom-call(s32[20,16]{1,0:T(8,128)S(1)} %reshape.21.index, f32[20,16]{1,0:T(8,128)S(1)} %reshape.22.weight, f32[128,8,256]{2,1,0:T(8,128)S(1)} %bitcast.19, f32[16,8,256]{2,1,0:T(8,128)S(1)} %bitcast.18, f32[16,8,256]{2,1,0:T(8,128)S(1)} %bitcast.20, f32[11,8,256]{2,1,0:T(8,128)S(1)} %pad_maximum_fusion.mid, ...), custom_call_target="tpu_custom_call" | custom-call | flops 5767168 | bytes 3252224 | tf_op jit(solution)/shard_map/pallas_call | solution.py:169
  44.5 17.4 %all_to_all.16.got = f32[16,4,8,256]{3,2,1,0:T(8,128)S(1)} all-to-all(f32[16,4,8,256]{3,2,1,0:T(8,128)S(1)} %shard_map.78), channel_id=1, replica_groups=mesh['gx'=16,'ma'=16] {'gx'}, dimensions={0} | all-to-all | bytes 1048576 | tf_op jit(solution)/shard_map/all_to_all | solution.py:173
  61.9 0.5 shard_map.79
  62.4 14.8 %all_to_all.17 = f32[16,2,8,256]{3,2,1,0:T(8,128)S(1)} all-to-all(f32[16,2,8,256]{3,2,1,0:T(8,128)S(1)} %shard_map.79), channel_id=1, replica_groups=mesh['gx'=16,'ma'=16] {'gx'}, dimensions={0} | all-to-all | bytes 524288 | tf_op jit(solution)/shard_map/all_to_all | solution.py:179
  77.2 0.7 fusion
  (12 shorter events, 0.1 us)
Async XLA Ops:
  0.6 31.1 %copy-start = (s32[256,10]{0,1:T(8,128)S(1)}, s32[256,10]{0,1:T(8,128)}, u32[]{:S(2)}) copy-start(s32[256,10]{0,1:T(8,128)} %param.11) | copy-start | bytes 30724
  1.6 23.3 %copy-start.3 = (f32[10,1,8,256]{3,2,1,0:T(8,128)S(1)}, f32[10,1,8,256]{3,2,1,0:T(8,128)}, u32[]{:S(2)}) copy-start(f32[10,1,8,256]{3,2,1,0:T(8,128)} %param.9) | copy-start | bytes 245764
  1.7 23.3 %copy-start.5 = (f32[1,8,256]{2,1,0:T(8,128)S(1)}, f32[1,8,256]{2,1,0:T(8,128)}, u32[]{:S(2)}) copy-start(f32[1,8,256]{2,1,0:T(8,128)} %param.8) | copy-start | bytes 24580
  24.9 15.7 %collective-permute-start = (f32[8,16,8,256]{3,2,1,0:T(8,128)S(1)}, f32[8,16,8,256]{3,2,1,0:T(8,128)S(1)}, u32[]{:S(2)}, u32[]{:S(2)}) collective-permute-start(f32[8,16,8,256]{3,2,1,0:T(8,128)S(1)} %all_to_all.15), channel_id=1, source_target_pairs={{0,1},{1,0},{2,3},{3,2},{4,5},{5,4},{6,7},{7,6},{8,9},{9,8},{10,11... | collective-permute-start | bytes 3145736 | tf_op jit(solution)/shard_map/ppermute | solution.py:148
  24.9 6.9 %copy-start.4 = (s32[10,256,2]{1,2,0:T(2,128)S(1)}, s32[10,256,2]{1,2,0:T(2,128)}, u32[]{:S(2)}) copy-start(s32[10,256,2]{1,2,0:T(2,128)} %param.10) | copy-start | bytes 61444
  25.0 13.6 %copy-start.1 = (f32[16,1,8,256]{3,2,1,0:T(8,128)S(1)}, f32[16,1,8,256]{3,2,1,0:T(8,128)}, u32[]{:S(2)}) copy-start(f32[16,1,8,256]{3,2,1,0:T(8,128)} %param.6) | copy-start | bytes 393220
  25.0 9.2 %collective-permute-start.1 = (f32[11,8,256]{2,1,0:T(8,128)S(1)}, f32[11,8,256]{2,1,0:T(8,128)S(1)}, u32[]{:S(2)}, u32[]{:S(2)}) collective-permute-start(f32[11,8,256]{2,1,0:T(8,128)S(1)} %pad_maximum_fusion.mid), channel_id=1, source_target_pairs={{16,0},{32,16},{48,32},{64,48},{80,64},{96,80},{112,96},{128,112},... | collective-permute-start | bytes 270344 | tf_op jit(solution)/shard_map/ppermute | solution.py:143
  31.7 6.8 %collective-permute-start.2 = (f32[11,8,256]{2,1,0:T(8,128)S(1)}, f32[11,8,256]{2,1,0:T(8,128)S(1)}, u32[]{:S(2)}, u32[]{:S(2)}) collective-permute-start(f32[11,8,256]{2,1,0:T(8,128)S(1)} %pad_maximum_fusion.mid), channel_id=1, source_target_pairs={{0,16},{16,32},{32,48},{48,64},{64,80},{80,96},{96,112},{112,128},... | collective-permute-start | bytes 270344 | tf_op jit(solution)/shard_map/ppermute | solution.py:142
  38.5 2.1 %copy-start.2 = (f32[16,1,8,256]{3,2,1,0:T(8,128)S(1)}, f32[16,1,8,256]{3,2,1,0:T(8,128)}, u32[]{:S(2)}) copy-start(f32[16,1,8,256]{3,2,1,0:T(8,128)} %param.7) | copy-start | bytes 393220

commit v3 on v2

--- a/solution.py
+++ b/solution.py
@@ -27,9 +27,8 @@
     return mixed
 
 
-def near_kernel(index, weight, near, sol, mid, up, down, sums, faces):
-    fields = mid.shape[0]
-    for q in range(fields):
+def face_kernel(mid, up, down, faces):
+    for q in range(mid.shape[0]):
         center = mid[q]
         faces[q, 0] = 0.5 * (center + up[q])
         faces[q, 1] = 0.5 * (center + down[q])
@@ -38,19 +37,21 @@
             faces[q, d] = face
             faces[q, d + 1] = behind(face, axis)
 
-    @pl.loop(0, sol.shape[0])
+
+def near_kernel(index, weight, near, sol, faces, sums):
+    @pl.loop(0, sol.shape[0], unroll=2)
     def _(i):
         value = sol[i]
         parts = [faces[0, d] * value for d in range(6)]
-        for k in range(fields - 1):
+        for k in range(faces.shape[0] - 1):
             mixed = mixture(index, weight, near, k, i)
             parts = [parts[d] + faces[k + 1, d] * mixed for d in range(6)]
         for d in range(6):
             sums[i, d] = parts[d]
 
 
-def far_kernel(index, weight, far, sol, src, mid, sums, faces, out):
-    @pl.loop(0, sol.shape[0])
+def far_kernel(index, weight, far, sol, src, sums, faces, out):
+    @pl.loop(0, sol.shape[0], unroll=4)
     def _(i):
         parts = [sums[i, d] for d in range(6)]
         for k in range(faces.shape[0] - 1):
@@ -63,16 +64,20 @@
         out[i, 0] = src[i] - image
         out[i, 1] = parts[0]
         out[i, 2] = parts[1]
-        out[i, 3] = mid[0]
-
-
-def cheb_kernel(got, out, faces, direction, remain):
+
+
+def cheb_kernel(place, got, near_mean, far_mean, out, mean, faces, direction, remain):
     planes = got.shape[0]
+    split = near_mean.shape[0]
     for x in range(planes):
-        center = got[x, 3]
-        faces[x, 0] = 0.5 * (center + got[(x + 1) % planes, 3])
+        mean[place[x]] = near_mean[x] if x < split else far_mean[x - split]
+    center = mean[0]
+    for x in range(planes):
+        after = mean[(x + 1) % planes]
+        faces[x, 0] = 0.5 * (center + after)
         faces[x, 1] = 0.5 * (center + ahead(center, 0))
         faces[x, 2] = 0.5 * (center + ahead(center, 1))
+        center = after
     theta = 13.0
     delta = 12.0
     sigma = theta / delta
@@ -138,9 +143,11 @@
     mid = jnp.concatenate([mean_conductivity, kl_fields[:, 0]], 0)
     fields = mid.shape[0]
 
-    ring = [(i, (i + 1) % planes) for i in range(planes)]
-    down = lax.ppermute(mid, "gx", ring)
-    up = lax.ppermute(mid, "gx", [(j, i) for i, j in ring])
+    def shifted(array, hops):
+        return lax.ppermute(array, "gx", [(i, (i + hops) % planes) for i in range(planes)])
+
+    down = shifted(mid, 1)
+    up = shifted(mid, -1)
 
     same_core = [[2 * chip + c for chip in range(chips)] for c in range(2)]
     spread = jnp.broadcast_to(sol[None], (chips,) + sol.shape)
@@ -162,20 +169,29 @@
     tile = (ny, nz)
     cell = ny * nz
     pool = (chips * modes,) + tile
-    sums, faces = kernel_of(
-        near_kernel, (f32(modes, 6, *tile), f32(fields, 6, *tile)), [SMEM] * 2 + [VMEM] * 5,
-        flops=modes * fields * 16 * cell, size=4 * cell * (chips * modes + 8 * modes + 9 * fields),
-    )(index, near_weight, near.reshape(pool), sol, mid, up, down)
+    faces = kernel_of(
+        face_kernel, f32(fields, 6, *tile), [VMEM] * 3, flops=fields * 10 * cell, size=4 * cell * 9 * fields
+    )(mid, up, down)
+    sums = kernel_of(
+        near_kernel, f32(modes, 6, *tile), [SMEM] * 2 + [VMEM] * 3,
+        flops=modes * fields * 16 * cell, size=4 * cell * (chips * modes + 8 * modes + 6 * fields),
+    )(index, near_weight, near.reshape(pool), sol, faces)
     mixed = kernel_of(
-        far_kernel, f32(modes, 4, *tile), [SMEM] * 2 + [VMEM] * 6,
-        flops=modes * fields * 16 * cell, size=4 * cell * (chips * modes + 12 * modes + 7 * fields),
-    )(index, far_weight, far.reshape(pool), sol, src, mid, sums, faces)
+        far_kernel, f32(modes, 3, *tile), [SMEM] * 2 + [VMEM] * 5,
+        flops=modes * fields * 16 * cell, size=4 * cell * (chips * modes + 11 * modes + 6 * fields),
+    )(index, far_weight, far.reshape(pool), sol, src, sums, faces)
+    three = jnp.concatenate([down[:1], mid[:1], up[:1]], 0)
+    low = shifted(three, 3)
+    high = shifted(three, -3)
+    nine = jnp.concatenate([low, three, high], 0)
+    rest = shifted(nine[1:8], planes // 2)
+    place = lax.rem(lax.iota(jnp.int32, planes) + (lax.axis_index("gx") + planes - 4), planes)
     got = lax.all_to_all(mixed, "gx", 0, 0, tiled=True)
     done = kernel_of(
-        cheb_kernel, f32(planes, 2, *tile), [VMEM],
-        [VMEM((planes, 3) + tile, jnp.float32), VMEM((2, planes) + tile, jnp.float32), VMEM((planes,) + tile, jnp.float32)],
+        cheb_kernel, f32(planes, 2, *tile), [SMEM] + [VMEM] * 3,
+        [VMEM((planes,) + tile, jnp.float32), VMEM((planes, 3) + tile, jnp.float32), VMEM((2, planes) + tile, jnp.float32), VMEM((planes,) + tile, jnp.float32)],
         flops=planes * STEPS * 30 * cell, size=4 * cell * planes * 6,
-    )(got)
+    )(place, got, nine, rest)
     back = lax.all_to_all(done, "gx", 0, 0, tiled=True)
     return (back[:, 0:1], back[:, 1:2])
 

time: 78.4 us -> 76.7 us (0.978)
  blocking collectives: 55.4 us -> 14.2 us
  starting transfers between devices: 6.72 us -> 26.6 us
  waiting for transfers between devices: 6.4 us -> 24.6 us
  local copies, waits for them, and re-layouts: 1.86 us -> 3.48 us
    all_to_all x2 -> x0, blocking collectives: 40.6 us -> none  [the longest x1 23.3 us: step(): lax.all_to_all(spread, 'ma', 0, 0, tiled=True, axis_index_groups=same_core)]
    all_to_all x0 -> x2, waiting for transfers between devices: none -> 18.3 us  [the longest x1 12.2 us: step(): lax.all_to_all(spread, 'ma', 0, 0, tiled=True, axis_index_groups=same_core)]
    all_to_all x0 -> x2, starting transfers between devices: none -> 13.4 us  [the longest x1 7.26 us: step(): got = lax.all_to_all(mixed, 'gx', 0, 0, tiled=True)]
    ppermute x2 -> x5, starting transfers between devices: 6.72 us -> 13.2 us  [shifted(): lax.ppermute(array, 'gx', [(i, (i + hops) % planes) for i in range(planes)])]
    broadcast_in_dim x1, local copies, waits for them, and re-layouts: 0.99 us -> 1.98 us  [step(): spread = jnp.broadcast_to(sol[None], (chips,) + sol.shape)]
    pallas_call x3 -> x4, Pallas kernels: 6.45 us -> 5.96 us  [the longest x1 2.88 us: step(): kernel_of(far_kernel, f32(modes, 3, *tile), [SMEM] * 2 + [VMEM] * 5, flop...]
    ppermute x2 -> x5, waiting for transfers between devices: 6.4 us -> 6.3 us  [shifted(): lax.ppermute(array, 'gx', [(i, (i + hops) % planes) for i in range(planes)])]
  transfers between devices with their start and end apart: 3 -> 8, of which waited for: 2 -> 4; matrix products, arithmetic and copies ran while one was open for 1% -> 1% of each run, Pallas kernels for 3% -> 6%
where the time goes in v3:
time: 76.7 us; the launch traced here: 76 us
  starting transfers between devices  26.6 us (35%)
  waiting for transfers between devices  24.6 us (32%)
  blocking collectives  14.2 us (19%)
  Pallas kernels  5.96 us (8%)
  local copies, waits for them, and re-layouts  3.48 us (5%)
  between operations  0.86 us (1%)
    all_to_all x1, blocking collectives, step(): back = lax.all_to_all(done, 'gx', 0, 0, tiled=True)  14.2 us
    ppermute x5, starting transfers between devices, shifted(): lax.ppermute(array, 'gx', [(i, (i + hops) % planes) for i in range(planes)])  13.2 us
    all_to_all x1, waiting for transfers between devices, step(): lax.all_to_all(spread, 'ma', 0, 0, tiled=True, axis_index_groups=same_core)  12.2 us
    all_to_all x1, starting transfers between devices, step(): got = lax.all_to_all(mixed, 'gx', 0, 0, tiled=True)  7.26 us
    ppermute x5, waiting for transfers between devices, shifted(): lax.ppermute(array, 'gx', [(i, (i + hops) % planes) for i in range(planes)])  6.3 us
    all_to_all x1, starting transfers between devices, step(): lax.all_to_all(spread, 'ma', 0, 0, tiled=True, axis_index_groups=same_core)  6.16 us
    all_to_all x1, waiting for transfers between devices, step(): got = lax.all_to_all(mixed, 'gx', 0, 0, tiled=True)  6.07 us
    pallas_call x1, Pallas kernels, step(): kernel_of(far_kernel, f32(modes, 3, *tile), [SMEM] * 2 + [VMEM] * 5, flop...  2.88 us
  transfers between devices with their start and end apart: 8, of which 4 were waited for; matrix products, arithmetic and copies ran while one was open for 1% of the time, Pallas kernels for 6%

profile of v3, /device:TPU:2, one launch (start us, length us, event | category | flops | bytes accessed | tf_op | source)
XLA Modules:
  0.0 76.0 jit_solution(1823682549710033458)
XLA Ops:
  0.6 0.0 copy-start
  0.6 2.0 %broadcast_in_dim.17 = f32[8,16,8,256]{3,2,1,0:T(8,128)} broadcast(f32[16,8,256]{2,1,0:T(8,128)} %bitcast.16), dimensions={1,2,3} | broadcast | bytes 1179648 | tf_op jit(solution)/shard_map/broadcast_in_dim | solution.py:153
  2.6 6.2 %all-to-all-start = ((f32[8,16,8,256]{3,2,1,0:T(8,128)}), f32[8,16,8,256]{3,2,1,0:T(8,128)S(1)}, u32[]{:S(2)}, u32[]{:S(2)}) async-start(f32[8,16,8,256]{3,2,1,0:T(8,128)} %broadcast_in_dim.17), calls=%async_computation | async-start | bytes 2097152 | tf_op jit(solution)/shard_map/all_to_all | solution.py:154
  8.8 2.0 %collective-permute-start.2 = (f32[11,8,256]{2,1,0:T(8,128)S(1)}, f32[11,8,256]{2,1,0:T(8,128)S(1)}, u32[]{:S(2)}, u32[]{:S(2)}) collective-permute-start(f32[11,8,256]{2,1,0:T(8,128)S(1)} %pad_maximum_fusion.mid), channel_id=1, source_target_pairs={{0,16},{16,32},{32,48},{48,64},{64,80},{80,96},{96,112},{112,128},... | collective-permute-start | bytes 270344 | tf_op jit(solution)/shard_map/ppermute | solution.py:147
  10.8 4.9 %collective-permute-start.1 = (f32[11,8,256]{2,1,0:T(8,128)S(1)}, f32[11,8,256]{2,1,0:T(8,128)S(1)}, u32[]{:S(2)}, u32[]{:S(2)}) collective-permute-start(f32[11,8,256]{2,1,0:T(8,128)S(1)} %pad_maximum_fusion.mid), channel_id=1, source_target_pairs={{0,240},{16,0},{32,16},{48,32},{64,48},{80,64},{96,80},{112,96},{1... | collective-permute-start | bytes 270344 | tf_op jit(solution)/shard_map/ppermute | solution.py:147
  15.7 12.2 %all-to-all-done = f32[8,16,8,256]{3,2,1,0:T(8,128)S(1)} async-done(((f32[8,16,8,256]{3,2,1,0:T(8,128)}), f32[8,16,8,256]{3,2,1,0:T(8,128)S(1)}, u32[]{:S(2)}, u32[]{:S(2)}) %all-to-all-start) | async-done | bytes 1048608 | tf_op jit(solution)/shard_map/all_to_all | solution.py:154
  28.0 0.1 dynamic-slice_bitcast_fusion
  28.1 0.6 copy-done.5
  28.7 0.1 bitcast_select_fusion.1
  28.8 0.1 bitcast_select_fusion.2
  28.9 2.8 %collective-permute-start.3 = (f32[3,8,256]{2,1,0:T(8,128)S(1)}, f32[3,8,256]{2,1,0:T(8,128)S(1)}, u32[]{:S(2)}, u32[]{:S(2)}) collective-permute-start(f32[3,8,256]{2,1,0:T(8,128)S(1)} %pad_maximum_fusion.1), channel_id=1, source_target_pairs={{0,48},{16,64},{32,80},{48,96},{64,112},{80,128},{96,144},{112,160... | collective-permute-start | bytes 73736 | tf_op jit(solution)/shard_map/ppermute | solution.py:147
  31.7 0.1 add_bitcast_fusion
  31.8 3.3 %collective-permute-start.4 = (f32[3,8,256]{2,1,0:T(8,128)S(1)}, f32[3,8,256]{2,1,0:T(8,128)S(1)}, u32[]{:S(2)}, u32[]{:S(2)}) collective-permute-start(f32[3,8,256]{2,1,0:T(8,128)S(1)} %pad_maximum_fusion.1), channel_id=1, source_target_pairs={{0,208},{16,224},{32,240},{48,0},{64,16},{80,32},{96,48},{112,64},... | collective-permute-start | bytes 73736 | tf_op jit(solution)/shard_map/ppermute | solution.py:147
  35.1 0.2 shard_map.77.faces
  35.3 1.4 %collective-permute-done.3 = f32[3,8,256]{2,1,0:T(8,128)S(1)} collective-permute-done((f32[3,8,256]{2,1,0:T(8,128)S(1)}, f32[3,8,256]{2,1,0:T(8,128)S(1)}, u32[]{:S(2)}, u32[]{:S(2)}) %collective-permute-start.3) | collective-permute-done | bytes 24608 | tf_op jit(solution)/shard_map/ppermute | solution.py:147
  36.7 1.8 %shard_map.78.sums = f32[16,6,8,256]{3,2,1,0:T(8,128)S(1)} custom-call(s32[20,16]{1,0:T(8,128)S(1)} %reshape.21.index, f32[20,16]{1,0:T(8,128)S(1)} %reshape.24.weight, f32[128,8,256]{2,1,0:T(8,128)S(1)} %bitcast.15, f32[16,8,256]{2,1,0:T(8,128)S(1)} %bitcast.17, f32[11,6,8,256]{3,2,1,0:T(8,128)S(1)} %shard_map.77.faces), custom_call_target="tpu_custom_call" | custom-call | flops 5767168 | bytes 2637824 | tf_op jit(solution)/shard_map/pallas_call | solution.py:175
  38.6 2.9 %shard_map.79 = f32[16,3,8,256]{3,2,1,0:T(8,128)} custom-call(s32[20,16]{1,0:T(8,128)S(1)} %reshape.21.index, f32[20,16]{1,0:T(8,128)S(1)} %reshape.22.weight, f32[128,8,256]{2,1,0:T(8,128)S(1)} %bitcast.19, f32[16,8,256]{2,1,0:T(8,128)S(1)} %bitcast.18, f32[16,8,256]{2,1,0:T(8,128)S(1)} %bitcast.20, f32[16,6,8,256]{3,2,1,0:T(8,128)S(1)} %shard_map.78.sums, ...), custom_call_target="tpu_custom_call" | custom-call | flops 5767168 | bytes 3031040 | tf_op jit(solution)/shard_map/pallas_call | solution.py:179
  41.5 7.3 %all-to-all-start.1 = ((f32[16,3,8,256]{3,2,1,0:T(8,128)}), f32[16,3,8,256]{3,2,1,0:T(8,128)S(1)}, u32[]{:S(2)}, u32[]{:S(2)}) async-start(f32[16,3,8,256]{3,2,1,0:T(8,128)} %shard_map.79), calls=%async_computation.1 | async-start | bytes 786432 | tf_op jit(solution)/shard_map/all_to_all | solution.py:189
  48.8 0.2 collective-permute-start.5
  49.0 4.9 %collective-permute-done.5.far_mean = f32[7,8,256]{2,1,0:T(8,128)S(1)} collective-permute-done((f32[7,8,256]{2,1,0:T(8,128)S(1)}, f32[7,8,256]{2,1,0:T(8,128)S(1)}, u32[]{:S(2)}, u32[]{:S(2)}) %collective-permute-start.5) | collective-permute-done | bytes 57376 | tf_op jit(solution)/shard_map/ppermute | solution.py:147
  53.9 6.1 %all-to-all-done.1.got = f32[16,3,8,256]{3,2,1,0:T(8,128)S(1)} async-done(((f32[16,3,8,256]{3,2,1,0:T(8,128)}), f32[16,3,8,256]{3,2,1,0:T(8,128)S(1)}, u32[]{:S(2)}, u32[]{:S(2)}) %all-to-all-start.1) | async-done | bytes 393248 | tf_op jit(solution)/shard_map/all_to_all | solution.py:189
  59.9 1.1 %shard_map.80 = f32[16,2,8,256]{3,2,1,0:T(8,128)S(1)} custom-call(s32[16]{0:T(128)S(1)} %compare_select_fusion.place, f32[16,3,8,256]{3,2,1,0:T(8,128)S(1)} %all-to-all-done.1.got, f32[9,8,256]{2,1,0:T(8,128)S(1)} %constant_dynamic-update-slice_fusion.near_mean, f32[7,8,256]{2,1,0:T(8,128)S(1)} %collective-permute-done.5.far_mean), custom_call_target="tpu_custom_call" | custom-call | flops 2949120 | bytes 786432 | tf_op jit(solution)/shard_map/pallas_call | solution.py:190
  61.0 14.2 %all_to_all.15 = f32[16,2,8,256]{3,2,1,0:T(8,128)S(1)} all-to-all(f32[16,2,8,256]{3,2,1,0:T(8,128)S(1)} %shard_map.80), channel_id=1, replica_groups=mesh['gx'=16,'ma'=16] {'gx'}, dimensions={0} | all-to-all | bytes 524288 | tf_op jit(solution)/shard_map/all_to_all | solution.py:195
  75.2 0.7 fusion.1
  (31 shorter events, 0.1 us)
Async XLA Ops:
  0.6 27.3 %copy-start = (s32[256,10]{0,1:T(8,128)S(1)}, s32[256,10]{0,1:T(8,128)}, u32[]{:S(2)}) copy-start(s32[256,10]{0,1:T(8,128)} %param.11) | copy-start | bytes 30724
  2.6 6.2 %copy-start.3 = (f32[10,1,8,256]{3,2,1,0:T(8,128)S(1)}, f32[10,1,8,256]{3,2,1,0:T(8,128)}, u32[]{:S(2)}) copy-start(f32[10,1,8,256]{3,2,1,0:T(8,128)} %param.9) | copy-start | bytes 245764
  2.6 6.2 %copy-start.4 = (f32[1,8,256]{2,1,0:T(8,128)S(1)}, f32[1,8,256]{2,1,0:T(8,128)}, u32[]{:S(2)}) copy-start(f32[1,8,256]{2,1,0:T(8,128)} %param.8) | copy-start | bytes 24580
  2.6 25.3 %all-to-all-start = ((f32[8,16,8,256]{3,2,1,0:T(8,128)}), f32[8,16,8,256]{3,2,1,0:T(8,128)S(1)}, u32[]{:S(2)}, u32[]{:S(2)}) async-start(f32[8,16,8,256]{3,2,1,0:T(8,128)} %broadcast_in_dim.17), calls=%async_computation | async-start | bytes 2097152 | tf_op jit(solution)/shard_map/all_to_all | solution.py:154
  8.8 20.0 %collective-permute-start.2 = (f32[11,8,256]{2,1,0:T(8,128)S(1)}, f32[11,8,256]{2,1,0:T(8,128)S(1)}, u32[]{:S(2)}, u32[]{:S(2)}) collective-permute-start(f32[11,8,256]{2,1,0:T(8,128)S(1)} %pad_maximum_fusion.mid), channel_id=1, source_target_pairs={{0,16},{16,32},{32,48},{48,64},{64,80},{80,96},{96,112},{112,128},... | collective-permute-start | bytes 270344 | tf_op jit(solution)/shard_map/ppermute | solution.py:147
  10.8 18.1 %collective-permute-start.1 = (f32[11,8,256]{2,1,0:T(8,128)S(1)}, f32[11,8,256]{2,1,0:T(8,128)S(1)}, u32[]{:S(2)}, u32[]{:S(2)}) collective-permute-start(f32[11,8,256]{2,1,0:T(8,128)S(1)} %pad_maximum_fusion.mid), channel_id=1, source_target_pairs={{0,240},{16,0},{32,16},{48,32},{64,48},{80,64},{96,80},{112,96},{1... | collective-permute-start | bytes 270344 | tf_op jit(solution)/shard_map/ppermute | solution.py:147
  27.9 10.6 %collective-permute-start = (f32[8,16,8,256]{3,2,1,0:T(8,128)S(1)}, f32[8,16,8,256]{3,2,1,0:T(8,128)S(1)}, u32[]{:S(2)}, u32[]{:S(2)}) collective-permute-start(f32[8,16,8,256]{3,2,1,0:T(8,128)S(1)} %all-to-all-done), channel_id=1, source_target_pairs={{0,1},{1,0},{2,3},{3,2},{4,5},{5,4},{6,7},{7,6},{8,9},{9,8},{10,11... | collective-permute-start | bytes 3145736 | tf_op jit(solution)/shard_map/ppermute | solution.py:155
  27.9 0.7 copy-start.5
  28.9 7.8 %collective-permute-start.3 = (f32[3,8,256]{2,1,0:T(8,128)S(1)}, f32[3,8,256]{2,1,0:T(8,128)S(1)}, u32[]{:S(2)}, u32[]{:S(2)}) collective-permute-start(f32[3,8,256]{2,1,0:T(8,128)S(1)} %pad_maximum_fusion.1), channel_id=1, source_target_pairs={{0,48},{16,64},{32,80},{48,96},{64,112},{80,128},{96,144},{112,160... | collective-permute-start | bytes 73736 | tf_op jit(solution)/shard_map/ppermute | solution.py:147
  31.8 16.9 %collective-permute-start.4 = (f32[3,8,256]{2,1,0:T(8,128)S(1)}, f32[3,8,256]{2,1,0:T(8,128)S(1)}, u32[]{:S(2)}, u32[]{:S(2)}) collective-permute-start(f32[3,8,256]{2,1,0:T(8,128)S(1)} %pad_maximum_fusion.1), channel_id=1, source_target_pairs={{0,208},{16,224},{32,240},{48,0},{64,16},{80,32},{96,48},{112,64},... | collective-permute-start | bytes 73736 | tf_op jit(solution)/shard_map/ppermute | solution.py:147
  35.1 1.6 %copy-start.1 = (f32[16,1,8,256]{3,2,1,0:T(8,128)S(1)}, f32[16,1,8,256]{3,2,1,0:T(8,128)}, u32[]{:S(2)}) copy-start(f32[16,1,8,256]{3,2,1,0:T(8,128)} %param.6) | copy-start | bytes 393220
  36.7 1.8 %copy-start.2 = (f32[16,1,8,256]{3,2,1,0:T(8,128)S(1)}, f32[16,1,8,256]{3,2,1,0:T(8,128)}, u32[]{:S(2)}) copy-start(f32[16,1,8,256]{3,2,1,0:T(8,128)} %param.7) | copy-start | bytes 393220
  41.5 18.5 %all-to-all-start.1 = ((f32[16,3,8,256]{3,2,1,0:T(8,128)}), f32[16,3,8,256]{3,2,1,0:T(8,128)S(1)}, u32[]{:S(2)}, u32[]{:S(2)}) async-start(f32[16,3,8,256]{3,2,1,0:T(8,128)} %shard_map.79), calls=%async_computation.1 | async-start | bytes 786432 | tf_op jit(solution)/shard_map/all_to_all | solution.py:189
  48.8 5.1 %collective-permute-start.5 = (f32[7,8,256]{2,1,0:T(8,128)S(1)}, f32[7,8,256]{2,1,0:T(8,128)S(1)}, u32[]{:S(2)}, u32[]{:S(2)}) collective-permute-start(f32[7,8,256]{2,1,0:T(8,128)S(1)} %slice.22), channel_id=1, source_target_pairs={{0,128},{16,144},{32,160},{48,176},{64,192},{80,208},{96,224},{112... | collective-permute-start | bytes 172040 | tf_op jit(solution)/shard_map/ppermute | solution.py:147

commit v4 on v3

--- a/solution.py
+++ b/solution.py
@@ -27,11 +27,12 @@
     return mixed
 
 
-def face_kernel(mid, up, down, faces):
+def face_kernel(mid, mine, theirs, faces):
+    first = lax.rem(lax.axis_index("ma"), 2) == 0
     for q in range(mid.shape[0]):
         center = mid[q]
-        faces[q, 0] = 0.5 * (center + up[q])
-        faces[q, 1] = 0.5 * (center + down[q])
+        faces[q, 0] = 0.5 * (center + jnp.where(first, theirs[q], mine[q]))
+        faces[q, 1] = 0.5 * (center + jnp.where(first, mine[q], theirs[q]))
         for d, axis in ((2, 0), (4, 1)):
             face = 0.5 * (center + ahead(center, axis))
             faces[q, d] = face
@@ -66,11 +67,12 @@
         out[i, 2] = parts[1]
 
 
-def cheb_kernel(place, got, near_mean, far_mean, out, mean, faces, direction, remain):
+def cheb_kernel(got, near_mean, far_mean, out, mean, faces, direction, remain):
     planes = got.shape[0]
     split = near_mean.shape[0]
+    first = lax.axis_index("gx") + planes - 4
     for x in range(planes):
-        mean[place[x]] = near_mean[x] if x < split else far_mean[x - split]
+        mean[lax.rem(first + x, planes)] = near_mean[x] if x < split else far_mean[x - split]
     center = mean[0]
     for x in range(planes):
         after = mean[(x + 1) % planes]
@@ -144,15 +146,26 @@
     fields = mid.shape[0]
 
     def shifted(array, hops):
-        return lax.ppermute(array, "gx", [(i, (i + hops) % planes) for i in range(planes)])
-
-    down = shifted(mid, 1)
-    up = shifted(mid, -1)
+        pairs = []
+        for x in range(planes):
+            for y in range(blocks):
+                target = (x + (hops if y % 2 == 0 else -hops)) % planes
+                pairs.append((x * blocks + y, target * blocks + y))
+        return lax.ppermute(array, ("gx", "ma"), pairs)
+
+    def swapped(array):
+        return lax.ppermute(array, "ma", [(i, i ^ 1) for i in range(blocks)])
+
+    def ordered(mine, theirs):
+        return jnp.where(core == 0, mine, theirs), jnp.where(core == 0, theirs, mine)
+
+    mine = shifted(mid, 1)
+    theirs = swapped(mine)
 
     same_core = [[2 * chip + c for chip in range(chips)] for c in range(2)]
     spread = jnp.broadcast_to(sol[None], (chips,) + sol.shape)
     near = lax.all_to_all(spread, "ma", 0, 0, tiled=True, axis_index_groups=same_core)
-    far = lax.ppermute(near, "ma", [(i, i ^ 1) for i in range(blocks)])
+    far = swapped(near)
 
     rows = lax.dynamic_slice_in_dim(couplings, block * modes, modes, 1).transpose(0, 2, 1)
     own = block * modes + lax.broadcasted_iota(jnp.int32, rows.shape, 2)
@@ -171,7 +184,7 @@
     pool = (chips * modes,) + tile
     faces = kernel_of(
         face_kernel, f32(fields, 6, *tile), [VMEM] * 3, flops=fields * 10 * cell, size=4 * cell * 9 * fields
-    )(mid, up, down)
+    )(mid, mine, theirs)
     sums = kernel_of(
         near_kernel, f32(modes, 6, *tile), [SMEM] * 2 + [VMEM] * 3,
         flops=modes * fields * 16 * cell, size=4 * cell * (chips * modes + 8 * modes + 6 * fields),
@@ -180,18 +193,19 @@
         far_kernel, f32(modes, 3, *tile), [SMEM] * 2 + [VMEM] * 5,
         flops=modes * fields * 16 * cell, size=4 * cell * (chips * modes + 11 * modes + 6 * fields),
     )(index, far_weight, far.reshape(pool), sol, src, sums, faces)
-    three = jnp.concatenate([down[:1], mid[:1], up[:1]], 0)
-    low = shifted(three, 3)
-    high = shifted(three, -3)
+    down, up = ordered(mine[:1], theirs[:1])
+    three = jnp.concatenate([down, mid[:1], up], 0)
+    mean_mine = shifted(three, 3)
+    mean_theirs = swapped(mean_mine)
+    low, high = ordered(mean_mine, mean_theirs)
     nine = jnp.concatenate([low, three, high], 0)
     rest = shifted(nine[1:8], planes // 2)
-    place = lax.rem(lax.iota(jnp.int32, planes) + (lax.axis_index("gx") + planes - 4), planes)
     got = lax.all_to_all(mixed, "gx", 0, 0, tiled=True)
     done = kernel_of(
-        cheb_kernel, f32(planes, 2, *tile), [SMEM] + [VMEM] * 3,
+        cheb_kernel, f32(planes, 2, *tile), [VMEM] * 3,
         [VMEM((planes,) + tile, jnp.float32), VMEM((planes, 3) + tile, jnp.float32), VMEM((2, planes) + tile, jnp.float32), VMEM((planes,) + tile, jnp.float32)],
         flops=planes * STEPS * 30 * cell, size=4 * cell * planes * 6,
-    )(place, got, nine, rest)
+    )(got, nine, rest)
     back = lax.all_to_all(done, "gx", 0, 0, tiled=True)
     return (back[:, 0:1], back[:, 1:2])
 

time: 76.7 us -> 80.8 us (1.053)
  waiting for transfers between devices: 24.6 us -> 35.2 us
  starting transfers between devices: 26.6 us -> 20.1 us
    ppermute x6, starting transfers between devices: 13.2 us -> 6.5 us  [the longest x3 5.91 us: shifted(): return lax.ppermute(array, ('gx', 'ma'), pairs)]
    ppermute x6, waiting for transfers between devices: 6.31 us -> 11.3 us  [the longest x3 9.19 us: shifted(): return lax.ppermute(array, ('gx', 'ma'), pairs)]
    all_to_all x1, waiting for transfers between devices: 12.2 us -> 16.1 us  [step(): lax.all_to_all(spread, 'ma', 0, 0, tiled=True, axis_index_groups=same_core)]
    all_to_all x1, waiting for transfers between devices: 6.07 us -> 7.88 us  [step(): got = lax.all_to_all(mixed, 'gx', 0, 0, tiled=True)]
  transfers between devices with their start and end apart: 8 -> 8, of which waited for: 4 -> 5; matrix products, arithmetic and copies ran while one was open for 1% -> 1% of each run, Pallas kernels for 6% -> 6%
where the time goes in v4:
time: 80.8 us; the launch traced here: 80.2 us
  waiting for transfers between devices  35.2 us (44%)
  starting transfers between devices  20.1 us (25%)
  blocking collectives  14.8 us (18%)
  Pallas kernels  5.42 us (7%)
  local copies, waits for them, and re-layouts  3.58 us (4%)
  between operations  0.82 us (1%)
    all_to_all x1, waiting for transfers between devices, step(): lax.all_to_all(spread, 'ma', 0, 0, tiled=True, axis_index_groups=same_core)  16.1 us
    all_to_all x1, blocking collectives, step(): back = lax.all_to_all(done, 'gx', 0, 0, tiled=True)  14.8 us
    ppermute x3, waiting for transfers between devices, shifted(): return lax.ppermute(array, ('gx', 'ma'), pairs)  9.19 us
    all_to_all x1, waiting for transfers between devices, step(): got = lax.all_to_all(mixed, 'gx', 0, 0, tiled=True)  7.88 us
    all_to_all x1, starting transfers between devices, step(): got = lax.all_to_all(mixed, 'gx', 0, 0, tiled=True)  7.46 us
    all_to_all x1, starting transfers between devices, step(): lax.all_to_all(spread, 'ma', 0, 0, tiled=True, axis_index_groups=same_core)  6.16 us
    ppermute x3, starting transfers between devices, shifted(): return lax.ppermute(array, ('gx', 'ma'), pairs)  5.91 us
    pallas_call x1, Pallas kernels, step(): kernel_of(far_kernel, f32(modes, 3, *tile), [SMEM] * 2 + [VMEM] * 5, flop...  2.88 us
  transfers between devices with their start and end apart: 8, of which 5 were waited for; matrix products, arithmetic and copies ran while one was open for 1% of the time, Pallas kernels for 6%

profile of v4, /device:TPU:2, one launch (start us, length us, event | category | flops | bytes accessed | tf_op | source)
XLA Modules:
  0.0 80.2 jit_solution(4368649817658450446)
XLA Ops:
  0.6 0.0 copy-start
  0.6 2.0 %broadcast_in_dim.17 = f32[8,16,8,256]{3,2,1,0:T(8,128)} broadcast(f32[16,8,256]{2,1,0:T(8,128)} %bitcast.16), dimensions={1,2,3} | broadcast | bytes 1179648 | tf_op jit(solution)/shard_map/broadcast_in_dim | solution.py:166
  2.6 6.2 %all-to-all-start = ((f32[8,16,8,256]{3,2,1,0:T(8,128)}), f32[8,16,8,256]{3,2,1,0:T(8,128)S(1)}, u32[]{:S(2)}, u32[]{:S(2)}) async-start(f32[8,16,8,256]{3,2,1,0:T(8,128)} %broadcast_in_dim.17), calls=%async_computation | async-start | bytes 2097152 | tf_op jit(solution)/shard_map/all_to_all | solution.py:167
  8.8 2.0 %collective-permute-start.1 = (f32[11,8,256]{2,1,0:T(8,128)S(1)}, f32[11,8,256]{2,1,0:T(8,128)S(1)}, u32[]{:S(2)}, u32[]{:S(2)}) collective-permute-start(f32[11,8,256]{2,1,0:T(8,128)S(1)} %pad_maximum_fusion.mid), channel_id=1, source_target_pairs={{0,16},{1,241},{2,18},{3,243},{4,20},{5,245},{6,22},{7,247},{8,24}... | collective-permute-start | bytes 270344 | tf_op jit(solution)/shard_map/ppermute | solution.py:154
  10.8 0.1 dynamic-slice_bitcast_fusion
  10.9 16.1 %all-to-all-done = f32[8,16,8,256]{3,2,1,0:T(8,128)S(1)} async-done(((f32[8,16,8,256]{3,2,1,0:T(8,128)}), f32[8,16,8,256]{3,2,1,0:T(8,128)S(1)}, u32[]{:S(2)}, u32[]{:S(2)}) %all-to-all-start) | async-done | bytes 1048608 | tf_op jit(solution)/shard_map/all_to_all | solution.py:167
  27.0 0.6 collective-permute-start.2
  27.6 0.1 bitcast_select_fusion.1
  27.7 2.1 %collective-permute-done.2.theirs = f32[11,8,256]{2,1,0:T(8,128)S(1)} collective-permute-done((f32[11,8,256]{2,1,0:T(8,128)S(1)}, f32[11,8,256]{2,1,0:T(8,128)S(1)}, u32[]{:S(2)}, u32[]{:S(2)}) %collective-permute-start.2) | collective-permute-done | bytes 90144 | tf_op jit(solution)/shard_map/ppermute | solution.py:157
  29.8 3.7 %collective-permute-start.3 = (f32[3,8,256]{2,1,0:T(8,128)S(1)}, f32[3,8,256]{2,1,0:T(8,128)S(1)}, u32[]{:S(2)}, u32[]{:S(2)}) collective-permute-start(f32[3,8,256]{2,1,0:T(8,128)S(1)} %pad_maximum_fusion.1), channel_id=1, source_target_pairs={{0,48},{1,209},{2,50},{3,211},{4,52},{5,213},{6,54},{7,215},{8,56}... | collective-permute-start | bytes 73736 | tf_op jit(solution)/shard_map/ppermute | solution.py:154
  33.5 0.1 bitcast_select_fusion.2
  33.6 4.7 %collective-permute-done.3 = f32[3,8,256]{2,1,0:T(8,128)S(1)} collective-permute-done((f32[3,8,256]{2,1,0:T(8,128)S(1)}, f32[3,8,256]{2,1,0:T(8,128)S(1)}, u32[]{:S(2)}, u32[]{:S(2)}) %collective-permute-start.3) | collective-permute-done | bytes 24608 | tf_op jit(solution)/shard_map/ppermute | solution.py:154
  38.3 0.1 add_bitcast_fusion
  38.5 0.2 shard_map.77.faces
  38.6 0.7 copy-done.1
  39.4 1.8 %shard_map.78.sums = f32[16,6,8,256]{3,2,1,0:T(8,128)S(1)} custom-call(s32[20,16]{1,0:T(8,128)S(1)} %reshape.21.index, f32[20,16]{1,0:T(8,128)S(1)} %reshape.24.weight, f32[128,8,256]{2,1,0:T(8,128)S(1)} %bitcast.15, f32[16,8,256]{2,1,0:T(8,128)S(1)} %bitcast.17, f32[11,6,8,256]{3,2,1,0:T(8,128)S(1)} %shard_map.77.faces), custom_call_target="tpu_custom_call" | custom-call | flops 5767168 | bytes 2637824 | tf_op jit(solution)/shard_map/pallas_call | solution.py:188
  41.2 2.9 %shard_map.79 = f32[16,3,8,256]{3,2,1,0:T(8,128)} custom-call(s32[20,16]{1,0:T(8,128)S(1)} %reshape.21.index, f32[20,16]{1,0:T(8,128)S(1)} %reshape.22.weight, f32[128,8,256]{2,1,0:T(8,128)S(1)} %bitcast.19, f32[16,8,256]{2,1,0:T(8,128)S(1)} %bitcast.18, f32[16,8,256]{2,1,0:T(8,128)S(1)} %bitcast.20, f32[16,6,8,256]{3,2,1,0:T(8,128)S(1)} %shard_map.78.sums, ...), custom_call_target="tpu_custom_call" | custom-call | flops 5767168 | bytes 3031040 | tf_op jit(solution)/shard_map/pallas_call | solution.py:192
  44.1 7.5 %all-to-all-start.1 = ((f32[16,3,8,256]{3,2,1,0:T(8,128)}), f32[16,3,8,256]{3,2,1,0:T(8,128)S(1)}, u32[]{:S(2)}, u32[]{:S(2)}) async-start(f32[16,3,8,256]{3,2,1,0:T(8,128)} %shard_map.79), calls=%async_computation.1 | async-start | bytes 786432 | tf_op jit(solution)/shard_map/all_to_all | solution.py:203
  51.6 0.2 collective-permute-start.5
  51.8 4.5 %collective-permute-done.5.far_mean = f32[7,8,256]{2,1,0:T(8,128)S(1)} collective-permute-done((f32[7,8,256]{2,1,0:T(8,128)S(1)}, f32[7,8,256]{2,1,0:T(8,128)S(1)}, u32[]{:S(2)}, u32[]{:S(2)}) %collective-permute-start.5) | collective-permute-done | bytes 57376 | tf_op jit(solution)/shard_map/ppermute | solution.py:154
  56.3 7.9 %all-to-all-done.1.got = f32[16,3,8,256]{3,2,1,0:T(8,128)S(1)} async-done(((f32[16,3,8,256]{3,2,1,0:T(8,128)}), f32[16,3,8,256]{3,2,1,0:T(8,128)S(1)}, u32[]{:S(2)}, u32[]{:S(2)}) %all-to-all-start.1) | async-done | bytes 393248 | tf_op jit(solution)/shard_map/all_to_all | solution.py:203
  64.1 0.6 shard_map.80
  64.7 14.8 %all_to_all.15 = f32[16,2,8,256]{3,2,1,0:T(8,128)S(1)} all-to-all(f32[16,2,8,256]{3,2,1,0:T(8,128)S(1)} %shard_map.80), channel_id=1, replica_groups=mesh['gx'=16,'ma'=16] {'gx'}, dimensions={0} | all-to-all | bytes 524288 | tf_op jit(solution)/shard_map/all_to_all | solution.py:209
  79.5 0.7 fusion
  (29 shorter events, 0.1 us)
Async XLA Ops:
  0.6 10.2 %copy-start = (s32[256,10]{0,1:T(8,128)S(1)}, s32[256,10]{0,1:T(8,128)}, u32[]{:S(2)}) copy-start(s32[256,10]{0,1:T(8,128)} %param.11) | copy-start | bytes 30724
  2.6 6.2 %copy-start.3 = (f32[10,1,8,256]{3,2,1,0:T(8,128)S(1)}, f32[10,1,8,256]{3,2,1,0:T(8,128)}, u32[]{:S(2)}) copy-start(f32[10,1,8,256]{3,2,1,0:T(8,128)} %param.9) | copy-start | bytes 245764
  2.6 6.2 %copy-start.4 = (f32[1,8,256]{2,1,0:T(8,128)S(1)}, f32[1,8,256]{2,1,0:T(8,128)}, u32[]{:S(2)}) copy-start(f32[1,8,256]{2,1,0:T(8,128)} %param.8) | copy-start | bytes 24580
  2.6 24.3 %all-to-all-start = ((f32[8,16,8,256]{3,2,1,0:T(8,128)}), f32[8,16,8,256]{3,2,1,0:T(8,128)S(1)}, u32[]{:S(2)}, u32[]{:S(2)}) async-start(f32[8,16,8,256]{3,2,1,0:T(8,128)} %broadcast_in_dim.17), calls=%async_computation | async-start | bytes 2097152 | tf_op jit(solution)/shard_map/all_to_all | solution.py:167
  8.8 18.2 %collective-permute-start.1 = (f32[11,8,256]{2,1,0:T(8,128)S(1)}, f32[11,8,256]{2,1,0:T(8,128)S(1)}, u32[]{:S(2)}, u32[]{:S(2)}) collective-permute-start(f32[11,8,256]{2,1,0:T(8,128)S(1)} %pad_maximum_fusion.mid), channel_id=1, source_target_pairs={{0,16},{1,241},{2,18},{3,243},{4,20},{5,245},{6,22},{7,247},{8,24}... | collective-permute-start | bytes 270344 | tf_op jit(solution)/shard_map/ppermute | solution.py:154
  10.8 16.8 %copy-start.5 = (s32[10,256,2]{1,2,0:T(2,128)S(1)}, s32[10,256,2]{1,2,0:T(2,128)}, u32[]{:S(2)}) copy-start(s32[10,256,2]{1,2,0:T(2,128)} %param.10) | copy-start | bytes 61444
  27.0 14.2 %collective-permute-start = (f32[8,16,8,256]{3,2,1,0:T(8,128)S(1)}, f32[8,16,8,256]{3,2,1,0:T(8,128)S(1)}, u32[]{:S(2)}, u32[]{:S(2)}) collective-permute-start(f32[8,16,8,256]{3,2,1,0:T(8,128)S(1)} %all-to-all-done), channel_id=1, source_target_pairs={{0,1},{1,0},{2,3},{3,2},{4,5},{5,4},{6,7},{7,6},{8,9},{9,8},{10,11... | collective-permute-start | bytes 3145736 | tf_op jit(solution)/shard_map/ppermute | solution.py:157
  27.0 2.8 %collective-permute-start.2 = (f32[11,8,256]{2,1,0:T(8,128)S(1)}, f32[11,8,256]{2,1,0:T(8,128)S(1)}, u32[]{:S(2)}, u32[]{:S(2)}) collective-permute-start(f32[11,8,256]{2,1,0:T(8,128)S(1)} %collective-permute-done.1.mine), channel_id=1, source_target_pairs={{0,1},{1,0},{2,3},{3,2},{4,5},{5,4},{6,7},{7,6},{8,9},{9,8},{10,11... | collective-permute-start | bytes 270344 | tf_op jit(solution)/shard_map/ppermute | solution.py:157
  29.8 8.5 %collective-permute-start.3 = (f32[3,8,256]{2,1,0:T(8,128)S(1)}, f32[3,8,256]{2,1,0:T(8,128)S(1)}, u32[]{:S(2)}, u32[]{:S(2)}) collective-permute-start(f32[3,8,256]{2,1,0:T(8,128)S(1)} %pad_maximum_fusion.1), channel_id=1, source_target_pairs={{0,48},{1,209},{2,50},{3,211},{4,52},{5,213},{6,54},{7,215},{8,56}... | collective-permute-start | bytes 73736 | tf_op jit(solution)/shard_map/ppermute | solution.py:154
  38.3 13.2 %collective-permute-start.4 = (f32[3,8,256]{2,1,0:T(8,128)S(1)}, f32[3,8,256]{2,1,0:T(8,128)S(1)}, u32[]{:S(2)}, u32[]{:S(2)}) collective-permute-start(f32[3,8,256]{2,1,0:T(8,128)S(1)} %collective-permute-done.3), channel_id=1, source_target_pairs={{0,1},{1,0},{2,3},{3,2},{4,5},{5,4},{6,7},{7,6},{8,9},{9,8},{10,11... | collective-permute-start | bytes 73736 | tf_op jit(solution)/shard_map/ppermute | solution.py:157
  38.4 0.9 %copy-start.1 = (f32[16,1,8,256]{3,2,1,0:T(8,128)S(1)}, f32[16,1,8,256]{3,2,1,0:T(8,128)}, u32[]{:S(2)}) copy-start(f32[16,1,8,256]{3,2,1,0:T(8,128)} %param.6) | copy-start | bytes 393220
  39.4 1.8 %copy-start.2 = (f32[16,1,8,256]{3,2,1,0:T(8,128)S(1)}, f32[16,1,8,256]{3,2,1,0:T(8,128)}, u32[]{:S(2)}) copy-start(f32[16,1,8,256]{3,2,1,0:T(8,128)} %param.7) | copy-start | bytes 393220
  44.1 20.1 %all-to-all-start.1 = ((f32[16,3,8,256]{3,2,1,0:T(8,128)}), f32[16,3,8,256]{3,2,1,0:T(8,128)S(1)}, u32[]{:S(2)}, u32[]{:S(2)}) async-start(f32[16,3,8,256]{3,2,1,0:T(8,128)} %shard_map.79), calls=%async_computation.1 | async-start | bytes 786432 | tf_op jit(solution)/shard_map/all_to_all | solution.py:203
  51.6 4.7 %collective-permute-start.5 = (f32[7,8,256]{2,1,0:T(8,128)S(1)}, f32[7,8,256]{2,1,0:T(8,128)S(1)}, u32[]{:S(2)}, u32[]{:S(2)}) collective-permute-start(f32[7,8,256]{2,1,0:T(8,128)S(1)} %slice.22), channel_id=1, source_target_pairs={{0,128},{1,129},{2,130},{3,131},{4,132},{5,133},{6,134},{7,135},{8... | collective-permute-start | bytes 172040 | tf_op jit(solution)/shard_map/ppermute | solution.py:154

commit v5 on v4

--- a/solution.py
+++ b/solution.py
@@ -39,32 +39,45 @@
             faces[q, d + 1] = behind(face, axis)
 
 
-def near_kernel(index, weight, near, sol, faces, sums):
-    @pl.loop(0, sol.shape[0], unroll=2)
-    def _(i):
-        value = sol[i]
-        parts = [faces[0, d] * value for d in range(6)]
-        for k in range(faces.shape[0] - 1):
-            mixed = mixture(index, weight, near, k, i)
-            parts = [parts[d] + faces[k + 1, d] * mixed for d in range(6)]
+def add_mixtures(index, weight, pool, faces, rows, parts):
+    for k in range(faces.shape[0] - 1):
+        mixed = [mixture(index, weight, pool, k, i) for i in rows]
         for d in range(6):
-            sums[i, d] = parts[d]
+            face = faces[k + 1, d]
+            for n in range(len(rows)):
+                parts[n][d] = parts[n][d] + face * mixed[n]
+    return parts
+
+
+def near_kernel(index, weight, near, faces, sums):
+    modes = sums.shape[0]
+    first = lax.div(lax.axis_index("ma"), 2) * modes
+
+    @pl.loop(0, modes // 2, unroll=8)
+    def _(pair):
+        rows = (2 * pair, 2 * pair + 1)
+        values = [near[first + i] for i in rows]
+        parts = [[faces[0, d] * value for d in range(6)] for value in values]
+        parts = add_mixtures(index, weight, near, faces, rows, parts)
+        for n, i in enumerate(rows):
+            for d in range(6):
+                sums[i, d] = parts[n][d]
 
 
 def far_kernel(index, weight, far, sol, src, sums, faces, out):
-    @pl.loop(0, sol.shape[0], unroll=4)
-    def _(i):
-        parts = [sums[i, d] for d in range(6)]
-        for k in range(faces.shape[0] - 1):
-            mixed = mixture(index, weight, far, k, i)
-            parts = [parts[d] + faces[k + 1, d] * mixed for d in range(6)]
-        image = sol[i]
-        for d, axis in ((2, 0), (4, 1)):
-            flux = parts[d] - ahead(parts[d + 1], axis)
-            image = image + (flux - behind(flux, axis))
-        out[i, 0] = src[i] - image
-        out[i, 1] = parts[0]
-        out[i, 2] = parts[1]
+    @pl.loop(0, sol.shape[0] // 2, unroll=8)
+    def _(pair):
+        rows = (2 * pair, 2 * pair + 1)
+        parts = [[sums[i, d] for d in range(6)] for i in rows]
+        parts = add_mixtures(index, weight, far, faces, rows, parts)
+        for n, i in enumerate(rows):
+            image = sol[i]
+            for d, axis in ((2, 0), (4, 1)):
+                flux = parts[n][d] - ahead(parts[n][d + 1], axis)
+                image = image + (flux - behind(flux, axis))
+            out[i, 0] = src[i] - image
+            out[i, 1] = parts[n][0]
+            out[i, 2] = parts[n][1]
 
 
 def cheb_kernel(got, near_mean, far_mean, out, mean, faces, direction, remain):
@@ -186,9 +199,9 @@
         face_kernel, f32(fields, 6, *tile), [VMEM] * 3, flops=fields * 10 * cell, size=4 * cell * 9 * fields
     )(mid, mine, theirs)
     sums = kernel_of(
-        near_kernel, f32(modes, 6, *tile), [SMEM] * 2 + [VMEM] * 3,
+        near_kernel, f32(modes, 6, *tile), [SMEM] * 2 + [VMEM] * 2,
         flops=modes * fields * 16 * cell, size=4 * cell * (chips * modes + 8 * modes + 6 * fields),
-    )(index, near_weight, near.reshape(pool), sol, faces)
+    )(index, near_weight, near.reshape(pool), faces)
     mixed = kernel_of(
         far_kernel, f32(modes, 3, *tile), [SMEM] * 2 + [VMEM] * 5,
         flops=modes * fields * 16 * cell, size=4 * cell * (chips * modes + 11 * modes + 6 * fields),

time: 80.8 us -> 79.8 us (0.988)
  no operation moved by 1% of the time
where the time goes in v5:
time: 79.8 us; the launch traced here: 79.2 us
  waiting for transfers between devices  35.2 us (44%)
  starting transfers between devices  20.1 us (25%)
  blocking collectives  14.8 us (19%)
  Pallas kernels  5.1 us (6%)
  local copies, waits for them, and re-layouts  2.85 us (4%)
  between operations  0.83 us (1%)
    all_to_all x1, waiting for transfers between devices, step(): lax.all_to_all(spread, 'ma', 0, 0, tiled=True, axis_index_groups=same_core)  16.1 us
    all_to_all x1, blocking collectives, step(): back = lax.all_to_all(done, 'gx', 0, 0, tiled=True)  14.8 us
    ppermute x3, waiting for transfers between devices, shifted(): return lax.ppermute(array, ('gx', 'ma'), pairs)  9.19 us
    all_to_all x1, waiting for transfers between devices, step(): got = lax.all_to_all(mixed, 'gx', 0, 0, tiled=True)  7.88 us
    all_to_all x1, starting transfers between devices, step(): got = lax.all_to_all(mixed, 'gx', 0, 0, tiled=True)  7.46 us
    all_to_all x1, starting transfers between devices, step(): lax.all_to_all(spread, 'ma', 0, 0, tiled=True, axis_index_groups=same_core)  6.16 us
    ppermute x3, starting transfers between devices, shifted(): return lax.ppermute(array, ('gx', 'ma'), pairs)  5.91 us
    pallas_call x1, Pallas kernels, step(): kernel_of(far_kernel, f32(modes, 3, *tile), [SMEM] * 2 + [VMEM] * 5, flop...  2.57 us
  transfers between devices with their start and end apart: 8, of which 5 were waited for; matrix products, arithmetic and copies ran while one was open for 1% of the time, Pallas kernels for 6%

profile of v5, /device:TPU:2, one launch (start us, length us, event | category | flops | bytes accessed | tf_op | source)
XLA Modules:
  0.0 79.2 jit_solution(12439318093685445052)
XLA Ops:
  0.6 0.0 copy-start
  0.6 2.0 %broadcast_in_dim.17 = f32[8,16,8,256]{3,2,1,0:T(8,128)} broadcast(f32[16,8,256]{2,1,0:T(8,128)} %bitcast.17), dimensions={1,2,3} | broadcast | bytes 1179648 | tf_op jit(solution)/shard_map/broadcast_in_dim | solution.py:179
  2.6 6.2 %all-to-all-start = ((f32[8,16,8,256]{3,2,1,0:T(8,128)}), f32[8,16,8,256]{3,2,1,0:T(8,128)S(1)}, u32[]{:S(2)}, u32[]{:S(2)}) async-start(f32[8,16,8,256]{3,2,1,0:T(8,128)} %broadcast_in_dim.17), calls=%async_computation | async-start | bytes 2097152 | tf_op jit(solution)/shard_map/all_to_all | solution.py:180
  8.8 2.0 %collective-permute-start.1 = (f32[11,8,256]{2,1,0:T(8,128)S(1)}, f32[11,8,256]{2,1,0:T(8,128)S(1)}, u32[]{:S(2)}, u32[]{:S(2)}) collective-permute-start(f32[11,8,256]{2,1,0:T(8,128)S(1)} %pad_maximum_fusion.mid), channel_id=1, source_target_pairs={{0,16},{1,241},{2,18},{3,243},{4,20},{5,245},{6,22},{7,247},{8,24}... | collective-permute-start | bytes 270344 | tf_op jit(solution)/shard_map/ppermute | solution.py:167
  10.8 0.1 dynamic-slice_bitcast_fusion
  10.9 16.1 %all-to-all-done = f32[8,16,8,256]{3,2,1,0:T(8,128)S(1)} async-done(((f32[8,16,8,256]{3,2,1,0:T(8,128)}), f32[8,16,8,256]{3,2,1,0:T(8,128)S(1)}, u32[]{:S(2)}, u32[]{:S(2)}) %all-to-all-start) | async-done | bytes 1048608 | tf_op jit(solution)/shard_map/all_to_all | solution.py:180
  27.0 0.6 collective-permute-start.2
  27.6 0.1 bitcast_select_fusion.1
  27.7 2.1 %collective-permute-done.2.theirs = f32[11,8,256]{2,1,0:T(8,128)S(1)} collective-permute-done((f32[11,8,256]{2,1,0:T(8,128)S(1)}, f32[11,8,256]{2,1,0:T(8,128)S(1)}, u32[]{:S(2)}, u32[]{:S(2)}) %collective-permute-start.2) | collective-permute-done | bytes 90144 | tf_op jit(solution)/shard_map/ppermute | solution.py:170
  29.8 3.7 %collective-permute-start.3 = (f32[3,8,256]{2,1,0:T(8,128)S(1)}, f32[3,8,256]{2,1,0:T(8,128)S(1)}, u32[]{:S(2)}, u32[]{:S(2)}) collective-permute-start(f32[3,8,256]{2,1,0:T(8,128)S(1)} %pad_maximum_fusion.1), channel_id=1, source_target_pairs={{0,48},{1,209},{2,50},{3,211},{4,52},{5,213},{6,54},{7,215},{8,56}... | collective-permute-start | bytes 73736 | tf_op jit(solution)/shard_map/ppermute | solution.py:167
  33.5 0.1 bitcast_select_fusion.2
  33.6 4.7 %collective-permute-done.3 = f32[3,8,256]{2,1,0:T(8,128)S(1)} collective-permute-done((f32[3,8,256]{2,1,0:T(8,128)S(1)}, f32[3,8,256]{2,1,0:T(8,128)S(1)}, u32[]{:S(2)}, u32[]{:S(2)}) %collective-permute-start.3) | collective-permute-done | bytes 24608 | tf_op jit(solution)/shard_map/ppermute | solution.py:167
  38.3 0.1 add_bitcast_fusion
  38.4 0.2 shard_map.77.faces
  38.6 0.0 copy-start.1
  38.6 1.8 %shard_map.78.sums = f32[16,6,8,256]{3,2,1,0:T(8,128)S(1)} custom-call(s32[20,16]{1,0:T(8,128)S(1)} %reshape.21.index, f32[20,16]{1,0:T(8,128)S(1)} %reshape.24.weight, f32[128,8,256]{2,1,0:T(8,128)S(1)} %bitcast.15, f32[11,6,8,256]{3,2,1,0:T(8,128)S(1)} %shard_map.77.faces), custom_call_target="tpu_custom_call" | custom-call | flops 5767168 | bytes 2637824 | tf_op jit(solution)/shard_map/pallas_call | solution.py:201
  40.5 2.6 %shard_map.79 = f32[16,3,8,256]{3,2,1,0:T(8,128)} custom-call(s32[20,16]{1,0:T(8,128)S(1)} %reshape.21.index, f32[20,16]{1,0:T(8,128)S(1)} %reshape.22.weight, f32[128,8,256]{2,1,0:T(8,128)S(1)} %bitcast.16, f32[16,8,256]{2,1,0:T(8,128)S(1)} %bitcast.18, f32[16,8,256]{2,1,0:T(8,128)S(1)} %bitcast.19, f32[16,6,8,256]{3,2,1,0:T(8,128)S(1)} %shard_map.78.sums, ...), custom_call_target="tpu_custom_call" | custom-call | flops 5767168 | bytes 3031040 | tf_op jit(solution)/shard_map/pallas_call | solution.py:205
  43.0 7.5 %all-to-all-start.1 = ((f32[16,3,8,256]{3,2,1,0:T(8,128)}), f32[16,3,8,256]{3,2,1,0:T(8,128)S(1)}, u32[]{:S(2)}, u32[]{:S(2)}) async-start(f32[16,3,8,256]{3,2,1,0:T(8,128)} %shard_map.79), calls=%async_computation.1 | async-start | bytes 786432 | tf_op jit(solution)/shard_map/all_to_all | solution.py:216
  50.6 0.2 collective-permute-start.5
  50.8 4.5 %collective-permute-done.5.far_mean = f32[7,8,256]{2,1,0:T(8,128)S(1)} collective-permute-done((f32[7,8,256]{2,1,0:T(8,128)S(1)}, f32[7,8,256]{2,1,0:T(8,128)S(1)}, u32[]{:S(2)}, u32[]{:S(2)}) %collective-permute-start.5) | collective-permute-done | bytes 57376 | tf_op jit(solution)/shard_map/ppermute | solution.py:167
  55.2 7.9 %all-to-all-done.1.got = f32[16,3,8,256]{3,2,1,0:T(8,128)S(1)} async-done(((f32[16,3,8,256]{3,2,1,0:T(8,128)}), f32[16,3,8,256]{3,2,1,0:T(8,128)S(1)}, u32[]{:S(2)}, u32[]{:S(2)}) %all-to-all-start.1) | async-done | bytes 393248 | tf_op jit(solution)/shard_map/all_to_all | solution.py:216
  63.1 0.6 shard_map.80
  63.7 14.8 %all_to_all.15 = f32[16,2,8,256]{3,2,1,0:T(8,128)S(1)} all-to-all(f32[16,2,8,256]{3,2,1,0:T(8,128)S(1)} %shard_map.80), channel_id=1, replica_groups=mesh['gx'=16,'ma'=16] {'gx'}, dimensions={0} | all-to-all | bytes 524288 | tf_op jit(solution)/shard_map/all_to_all | solution.py:222
  78.5 0.7 fusion
  (29 shorter events, 0.1 us)
Async XLA Ops:
  0.6 10.2 %copy-start = (s32[256,10]{0,1:T(8,128)S(1)}, s32[256,10]{0,1:T(8,128)}, u32[]{:S(2)}) copy-start(s32[256,10]{0,1:T(8,128)} %param.11) | copy-start | bytes 30724
  2.6 6.2 %copy-start.3 = (f32[10,1,8,256]{3,2,1,0:T(8,128)S(1)}, f32[10,1,8,256]{3,2,1,0:T(8,128)}, u32[]{:S(2)}) copy-start(f32[10,1,8,256]{3,2,1,0:T(8,128)} %param.9) | copy-start | bytes 245764
  2.6 6.2 %copy-start.4 = (f32[1,8,256]{2,1,0:T(8,128)S(1)}, f32[1,8,256]{2,1,0:T(8,128)}, u32[]{:S(2)}) copy-start(f32[1,8,256]{2,1,0:T(8,128)} %param.8) | copy-start | bytes 24580
  2.6 24.3 %all-to-all-start = ((f32[8,16,8,256]{3,2,1,0:T(8,128)}), f32[8,16,8,256]{3,2,1,0:T(8,128)S(1)}, u32[]{:S(2)}, u32[]{:S(2)}) async-start(f32[8,16,8,256]{3,2,1,0:T(8,128)} %broadcast_in_dim.17), calls=%async_computation | async-start | bytes 2097152 | tf_op jit(solution)/shard_map/all_to_all | solution.py:180
  8.8 18.2 %collective-permute-start.1 = (f32[11,8,256]{2,1,0:T(8,128)S(1)}, f32[11,8,256]{2,1,0:T(8,128)S(1)}, u32[]{:S(2)}, u32[]{:S(2)}) collective-permute-start(f32[11,8,256]{2,1,0:T(8,128)S(1)} %pad_maximum_fusion.mid), channel_id=1, source_target_pairs={{0,16},{1,241},{2,18},{3,243},{4,20},{5,245},{6,22},{7,247},{8,24}... | collective-permute-start | bytes 270344 | tf_op jit(solution)/shard_map/ppermute | solution.py:167
  10.8 16.8 %copy-start.5 = (s32[10,256,2]{1,2,0:T(2,128)S(1)}, s32[10,256,2]{1,2,0:T(2,128)}, u32[]{:S(2)}) copy-start(s32[10,256,2]{1,2,0:T(2,128)} %param.10) | copy-start | bytes 61444
  27.0 13.5 %collective-permute-start = (f32[8,16,8,256]{3,2,1,0:T(8,128)S(1)}, f32[8,16,8,256]{3,2,1,0:T(8,128)S(1)}, u32[]{:S(2)}, u32[]{:S(2)}) collective-permute-start(f32[8,16,8,256]{3,2,1,0:T(8,128)S(1)} %all-to-all-done), channel_id=1, source_target_pairs={{0,1},{1,0},{2,3},{3,2},{4,5},{5,4},{6,7},{7,6},{8,9},{9,8},{10,11... | collective-permute-start | bytes 3145736 | tf_op jit(solution)/shard_map/ppermute | solution.py:170
  27.0 2.8 %collective-permute-start.2 = (f32[11,8,256]{2,1,0:T(8,128)S(1)}, f32[11,8,256]{2,1,0:T(8,128)S(1)}, u32[]{:S(2)}, u32[]{:S(2)}) collective-permute-start(f32[11,8,256]{2,1,0:T(8,128)S(1)} %collective-permute-done.1.mine), channel_id=1, source_target_pairs={{0,1},{1,0},{2,3},{3,2},{4,5},{5,4},{6,7},{7,6},{8,9},{9,8},{10,11... | collective-permute-start | bytes 270344 | tf_op jit(solution)/shard_map/ppermute | solution.py:170
  29.8 8.5 %collective-permute-start.3 = (f32[3,8,256]{2,1,0:T(8,128)S(1)}, f32[3,8,256]{2,1,0:T(8,128)S(1)}, u32[]{:S(2)}, u32[]{:S(2)}) collective-permute-start(f32[3,8,256]{2,1,0:T(8,128)S(1)} %pad_maximum_fusion.1), channel_id=1, source_target_pairs={{0,48},{1,209},{2,50},{3,211},{4,52},{5,213},{6,54},{7,215},{8,56}... | collective-permute-start | bytes 73736 | tf_op jit(solution)/shard_map/ppermute | solution.py:167
  38.3 12.2 %collective-permute-start.4 = (f32[3,8,256]{2,1,0:T(8,128)S(1)}, f32[3,8,256]{2,1,0:T(8,128)S(1)}, u32[]{:S(2)}, u32[]{:S(2)}) collective-permute-start(f32[3,8,256]{2,1,0:T(8,128)S(1)} %collective-permute-done.3), channel_id=1, source_target_pairs={{0,1},{1,0},{2,3},{3,2},{4,5},{5,4},{6,7},{7,6},{8,9},{9,8},{10,11... | collective-permute-start | bytes 73736 | tf_op jit(solution)/shard_map/ppermute | solution.py:170
  38.6 1.8 %copy-start.1 = (f32[16,1,8,256]{3,2,1,0:T(8,128)S(1)}, f32[16,1,8,256]{3,2,1,0:T(8,128)}, u32[]{:S(2)}) copy-start(f32[16,1,8,256]{3,2,1,0:T(8,128)} %param.6) | copy-start | bytes 393220
  38.6 1.8 %copy-start.2 = (f32[16,1,8,256]{3,2,1,0:T(8,128)S(1)}, f32[16,1,8,256]{3,2,1,0:T(8,128)}, u32[]{:S(2)}) copy-start(f32[16,1,8,256]{3,2,1,0:T(8,128)} %param.7) | copy-start | bytes 393220
  43.0 20.1 %all-to-all-start.1 = ((f32[16,3,8,256]{3,2,1,0:T(8,128)}), f32[16,3,8,256]{3,2,1,0:T(8,128)S(1)}, u32[]{:S(2)}, u32[]{:S(2)}) async-start(f32[16,3,8,256]{3,2,1,0:T(8,128)} %shard_map.79), calls=%async_computation.1 | async-start | bytes 786432 | tf_op jit(solution)/shard_map/all_to_all | solution.py:216
  50.6 4.7 %collective-permute-start.5 = (f32[7,8,256]{2,1,0:T(8,128)S(1)}, f32[7,8,256]{2,1,0:T(8,128)S(1)}, u32[]{:S(2)}, u32[]{:S(2)}) collective-permute-start(f32[7,8,256]{2,1,0:T(8,128)S(1)} %slice.22), channel_id=1, source_target_pairs={{0,128},{1,129},{2,130},{3,131},{4,132},{5,133},{6,134},{7,135},{8... | collective-permute-start | bytes 172040 | tf_op jit(solution)/shard_map/ppermute | solution.py:167

commit v6 on v5

--- a/solution.py
+++ b/solution.py
@@ -64,9 +64,9 @@
                 sums[i, d] = parts[n][d]
 
 
-def far_kernel(index, weight, far, sol, src, sums, faces, out):
-    @pl.loop(0, sol.shape[0] // 2, unroll=8)
-    def _(pair):
+def far_kernel(index, weight, far, sol, src, sums, faces, out, held, sems):
+    writes = []
+    for pair in range(sol.shape[0] // 2):
         rows = (2 * pair, 2 * pair + 1)
         parts = [[sums[i, d] for d in range(6)] for i in rows]
         parts = add_mixtures(index, weight, far, faces, rows, parts)
@@ -75,9 +75,14 @@
             for d, axis in ((2, 0), (4, 1)):
                 flux = parts[n][d] - ahead(parts[n][d + 1], axis)
                 image = image + (flux - behind(flux, axis))
-            out[i, 0] = src[i] - image
-            out[i, 1] = parts[n][0]
-            out[i, 2] = parts[n][1]
+            held[i, 0] = src[i] - image
+            held[i, 1] = parts[n][0]
+            held[i, 2] = parts[n][1]
+        slab = pl.ds(2 * pair, 2)
+        writes.append(pltpu.make_async_copy(held.at[slab], out.at[slab], sems.at[pair]))
+        writes[-1].start()
+    for write in writes:
+        write.wait()
 
 
 def cheb_kernel(got, near_mean, far_mean, out, mean, faces, direction, remain):
@@ -130,12 +135,12 @@
     return pl.BlockSpec(memory_space=memory)
 
 
-def kernel_of(body, outs, memories, scratch=(), flops=0, size=0):
+def kernel_of(body, outs, memories, scratch=(), flops=0, size=0, out_memory=VMEM):
     return pl.pallas_call(
         body,
         out_shape=outs,
         in_specs=[whole(m) for m in memories],
-        out_specs=jax.tree.map(lambda _: whole(VMEM), outs),
+        out_specs=jax.tree.map(lambda _: whole(out_memory), outs),
         scratch_shapes=list(scratch),
         compiler_params=pltpu.CompilerParams(vmem_limit_bytes=8 << 20),
         cost_estimate=pl.CostEstimate(flops=flops, bytes_accessed=size, transcendentals=0),
@@ -204,6 +209,7 @@
     )(index, near_weight, near.reshape(pool), faces)
     mixed = kernel_of(
         far_kernel, f32(modes, 3, *tile), [SMEM] * 2 + [VMEM] * 5,
+        [VMEM((modes, 3) + tile, jnp.float32), pltpu.SemaphoreType.DMA((modes // 2,))], out_memory=pl.ANY,
         flops=modes * fields * 16 * cell, size=4 * cell * (chips * modes + 11 * modes + 6 * fields),
     )(index, far_weight, far.reshape(pool), sol, src, sums, faces)
     down, up = ordered(mine[:1], theirs[:1])

time: 79.8 us -> 79.7 us (level)
  no operation moved by 1% of the time
where the time goes in v6:
time: 79.7 us; the launch traced here: 79.2 us
  waiting for transfers between devices  35.2 us (44%)
  starting transfers between devices  20.1 us (25%)
  blocking collectives  14.8 us (19%)
  Pallas kernels  5.02 us (6%)
  local copies, waits for them, and re-layouts  2.85 us (4%)
  between operations  0.84 us (1%)
    all_to_all x1, waiting for transfers between devices, step(): lax.all_to_all(spread, 'ma', 0, 0, tiled=True, axis_index_groups=same_core)  16.1 us
    all_to_all x1, blocking collectives, step(): back = lax.all_to_all(done, 'gx', 0, 0, tiled=True)  14.8 us
    ppermute x3, waiting for transfers between devices, shifted(): return lax.ppermute(array, ('gx', 'ma'), pairs)  9.19 us
    all_to_all x1, waiting for transfers between devices, step(): got = lax.all_to_all(mixed, 'gx', 0, 0, tiled=True)  7.88 us
    all_to_all x1, starting transfers between devices, step(): got = lax.all_to_all(mixed, 'gx', 0, 0, tiled=True)  7.47 us
    all_to_all x1, starting transfers between devices, step(): lax.all_to_all(spread, 'ma', 0, 0, tiled=True, axis_index_groups=same_core)  6.16 us
    ppermute x3, starting transfers between devices, shifted(): return lax.ppermute(array, ('gx', 'ma'), pairs)  5.91 us
    pallas_call x1, Pallas kernels, step(): kernel_of(far_kernel, f32(modes, 3, *tile), [SMEM] * 2 + [VMEM] * 5, [VME...  2.49 us
  transfers between devices with their start and end apart: 8, of which 5 were waited for; matrix products, arithmetic and copies ran while one was open for 1% of the time, Pallas kernels for 6%

profile of v6, /device:TPU:2, one launch (start us, length us, event | category | flops | bytes accessed | tf_op | source)
XLA Modules:
  0.0 79.2 jit_solution(14208899148536655335)
XLA Ops:
  0.6 0.0 copy-start
  0.6 2.0 %broadcast_in_dim.17 = f32[8,16,8,256]{3,2,1,0:T(8,128)} broadcast(f32[16,8,256]{2,1,0:T(8,128)} %bitcast.17), dimensions={1,2,3} | broadcast | bytes 1179648 | tf_op jit(solution)/shard_map/broadcast_in_dim | solution.py:184
  2.6 6.2 %all-to-all-start = ((f32[8,16,8,256]{3,2,1,0:T(8,128)}), f32[8,16,8,256]{3,2,1,0:T(8,128)S(1)}, u32[]{:S(2)}, u32[]{:S(2)}) async-start(f32[8,16,8,256]{3,2,1,0:T(8,128)} %broadcast_in_dim.17), calls=%async_computation | async-start | bytes 2097152 | tf_op jit(solution)/shard_map/all_to_all | solution.py:185
  8.8 2.0 %collective-permute-start.1 = (f32[11,8,256]{2,1,0:T(8,128)S(1)}, f32[11,8,256]{2,1,0:T(8,128)S(1)}, u32[]{:S(2)}, u32[]{:S(2)}) collective-permute-start(f32[11,8,256]{2,1,0:T(8,128)S(1)} %pad_maximum_fusion.mid), channel_id=1, source_target_pairs={{0,16},{1,241},{2,18},{3,243},{4,20},{5,245},{6,22},{7,247},{8,24}... | collective-permute-start | bytes 270344 | tf_op jit(solution)/shard_map/ppermute | solution.py:172
  10.8 0.1 dynamic-slice_bitcast_fusion
  10.9 16.1 %all-to-all-done = f32[8,16,8,256]{3,2,1,0:T(8,128)S(1)} async-done(((f32[8,16,8,256]{3,2,1,0:T(8,128)}), f32[8,16,8,256]{3,2,1,0:T(8,128)S(1)}, u32[]{:S(2)}, u32[]{:S(2)}) %all-to-all-start) | async-done | bytes 1048608 | tf_op jit(solution)/shard_map/all_to_all | solution.py:185
  27.0 0.6 collective-permute-start.2
  27.6 0.1 bitcast_select_fusion.1
  27.7 2.1 %collective-permute-done.2.theirs = f32[11,8,256]{2,1,0:T(8,128)S(1)} collective-permute-done((f32[11,8,256]{2,1,0:T(8,128)S(1)}, f32[11,8,256]{2,1,0:T(8,128)S(1)}, u32[]{:S(2)}, u32[]{:S(2)}) %collective-permute-start.2) | collective-permute-done | bytes 90144 | tf_op jit(solution)/shard_map/ppermute | solution.py:175
  29.8 3.7 %collective-permute-start.3 = (f32[3,8,256]{2,1,0:T(8,128)S(1)}, f32[3,8,256]{2,1,0:T(8,128)S(1)}, u32[]{:S(2)}, u32[]{:S(2)}) collective-permute-start(f32[3,8,256]{2,1,0:T(8,128)S(1)} %pad_maximum_fusion.1), channel_id=1, source_target_pairs={{0,48},{1,209},{2,50},{3,211},{4,52},{5,213},{6,54},{7,215},{8,56}... | collective-permute-start | bytes 73736 | tf_op jit(solution)/shard_map/ppermute | solution.py:172
  33.5 0.1 bitcast_select_fusion.2
  33.6 4.7 %collective-permute-done.3 = f32[3,8,256]{2,1,0:T(8,128)S(1)} collective-permute-done((f32[3,8,256]{2,1,0:T(8,128)S(1)}, f32[3,8,256]{2,1,0:T(8,128)S(1)}, u32[]{:S(2)}, u32[]{:S(2)}) %collective-permute-start.3) | collective-permute-done | bytes 24608 | tf_op jit(solution)/shard_map/ppermute | solution.py:172
  38.3 0.1 add_bitcast_fusion
  38.4 0.2 shard_map.77.faces
  38.6 0.0 copy-start.1
  38.6 1.8 %shard_map.78.sums = f32[16,6,8,256]{3,2,1,0:T(8,128)S(1)} custom-call(s32[20,16]{1,0:T(8,128)S(1)} %reshape.21.index, f32[20,16]{1,0:T(8,128)S(1)} %reshape.24.weight, f32[128,8,256]{2,1,0:T(8,128)S(1)} %bitcast.15, f32[11,6,8,256]{3,2,1,0:T(8,128)S(1)} %shard_map.77.faces), custom_call_target="tpu_custom_call" | custom-call | flops 5767168 | bytes 2637824 | tf_op jit(solution)/shard_map/pallas_call | solution.py:206
  40.5 2.5 %shard_map.79 = f32[16,3,8,256]{3,2,1,0:T(8,128)} custom-call(s32[20,16]{1,0:T(8,128)S(1)} %reshape.21.index, f32[20,16]{1,0:T(8,128)S(1)} %reshape.22.weight, f32[128,8,256]{2,1,0:T(8,128)S(1)} %bitcast.16, f32[16,8,256]{2,1,0:T(8,128)S(1)} %bitcast.18, f32[16,8,256]{2,1,0:T(8,128)S(1)} %bitcast.19, f32[16,6,8,256]{3,2,1,0:T(8,128)S(1)} %shard_map.78.sums, ...), custom_call_target="tpu_custom_call" | custom-call | flops 5767168 | bytes 3031040 | tf_op jit(solution)/shard_map/pallas_call | solution.py:210
  43.0 7.5 %all-to-all-start.1 = ((f32[16,3,8,256]{3,2,1,0:T(8,128)}), f32[16,3,8,256]{3,2,1,0:T(8,128)S(1)}, u32[]{:S(2)}, u32[]{:S(2)}) async-start(f32[16,3,8,256]{3,2,1,0:T(8,128)} %shard_map.79), calls=%async_computation.1 | async-start | bytes 786432 | tf_op jit(solution)/shard_map/all_to_all | solution.py:222
  50.5 0.2 collective-permute-start.5
  50.7 4.5 %collective-permute-done.5.far_mean = f32[7,8,256]{2,1,0:T(8,128)S(1)} collective-permute-done((f32[7,8,256]{2,1,0:T(8,128)S(1)}, f32[7,8,256]{2,1,0:T(8,128)S(1)}, u32[]{:S(2)}, u32[]{:S(2)}) %collective-permute-start.5) | collective-permute-done | bytes 57376 | tf_op jit(solution)/shard_map/ppermute | solution.py:172
  55.2 7.9 %all-to-all-done.1.got = f32[16,3,8,256]{3,2,1,0:T(8,128)S(1)} async-done(((f32[16,3,8,256]{3,2,1,0:T(8,128)}), f32[16,3,8,256]{3,2,1,0:T(8,128)S(1)}, u32[]{:S(2)}, u32[]{:S(2)}) %all-to-all-start.1) | async-done | bytes 393248 | tf_op jit(solution)/shard_map/all_to_all | solution.py:222
  63.1 0.6 shard_map.80
  63.6 14.8 %all_to_all.15 = f32[16,2,8,256]{3,2,1,0:T(8,128)S(1)} all-to-all(f32[16,2,8,256]{3,2,1,0:T(8,128)S(1)} %shard_map.80), channel_id=1, replica_groups=mesh['gx'=16,'ma'=16] {'gx'}, dimensions={0} | all-to-all | bytes 524288 | tf_op jit(solution)/shard_map/all_to_all | solution.py:228
  78.4 0.7 fusion
  (29 shorter events, 0.1 us)
Async XLA Ops:
  0.6 10.2 %copy-start = (s32[256,10]{0,1:T(8,128)S(1)}, s32[256,10]{0,1:T(8,128)}, u32[]{:S(2)}) copy-start(s32[256,10]{0,1:T(8,128)} %param.11) | copy-start | bytes 30724
  2.6 6.2 %copy-start.3 = (f32[10,1,8,256]{3,2,1,0:T(8,128)S(1)}, f32[10,1,8,256]{3,2,1,0:T(8,128)}, u32[]{:S(2)}) copy-start(f32[10,1,8,256]{3,2,1,0:T(8,128)} %param.9) | copy-start | bytes 245764
  2.6 6.2 %copy-start.4 = (f32[1,8,256]{2,1,0:T(8,128)S(1)}, f32[1,8,256]{2,1,0:T(8,128)}, u32[]{:S(2)}) copy-start(f32[1,8,256]{2,1,0:T(8,128)} %param.8) | copy-start | bytes 24580
  2.6 24.3 %all-to-all-start = ((f32[8,16,8,256]{3,2,1,0:T(8,128)}), f32[8,16,8,256]{3,2,1,0:T(8,128)S(1)}, u32[]{:S(2)}, u32[]{:S(2)}) async-start(f32[8,16,8,256]{3,2,1,0:T(8,128)} %broadcast_in_dim.17), calls=%async_computation | async-start | bytes 2097152 | tf_op jit(solution)/shard_map/all_to_all | solution.py:185
  8.8 18.2 %collective-permute-start.1 = (f32[11,8,256]{2,1,0:T(8,128)S(1)}, f32[11,8,256]{2,1,0:T(8,128)S(1)}, u32[]{:S(2)}, u32[]{:S(2)}) collective-permute-start(f32[11,8,256]{2,1,0:T(8,128)S(1)} %pad_maximum_fusion.mid), channel_id=1, source_target_pairs={{0,16},{1,241},{2,18},{3,243},{4,20},{5,245},{6,22},{7,247},{8,24}... | collective-permute-start | bytes 270344 | tf_op jit(solution)/shard_map/ppermute | solution.py:172
  10.8 16.8 %copy-start.5 = (s32[10,256,2]{1,2,0:T(2,128)S(1)}, s32[10,256,2]{1,2,0:T(2,128)}, u32[]{:S(2)}) copy-start(s32[10,256,2]{1,2,0:T(2,128)} %param.10) | copy-start | bytes 61444
  27.0 13.5 %collective-permute-start = (f32[8,16,8,256]{3,2,1,0:T(8,128)S(1)}, f32[8,16,8,256]{3,2,1,0:T(8,128)S(1)}, u32[]{:S(2)}, u32[]{:S(2)}) collective-permute-start(f32[8,16,8,256]{3,2,1,0:T(8,128)S(1)} %all-to-all-done), channel_id=1, source_target_pairs={{0,1},{1,0},{2,3},{3,2},{4,5},{5,4},{6,7},{7,6},{8,9},{9,8},{10,11... | collective-permute-start | bytes 3145736 | tf_op jit(solution)/shard_map/ppermute | solution.py:175
  27.0 2.8 %collective-permute-start.2 = (f32[11,8,256]{2,1,0:T(8,128)S(1)}, f32[11,8,256]{2,1,0:T(8,128)S(1)}, u32[]{:S(2)}, u32[]{:S(2)}) collective-permute-start(f32[11,8,256]{2,1,0:T(8,128)S(1)} %collective-permute-done.1.mine), channel_id=1, source_target_pairs={{0,1},{1,0},{2,3},{3,2},{4,5},{5,4},{6,7},{7,6},{8,9},{9,8},{10,11... | collective-permute-start | bytes 270344 | tf_op jit(solution)/shard_map/ppermute | solution.py:175
  29.8 8.5 %collective-permute-start.3 = (f32[3,8,256]{2,1,0:T(8,128)S(1)}, f32[3,8,256]{2,1,0:T(8,128)S(1)}, u32[]{:S(2)}, u32[]{:S(2)}) collective-permute-start(f32[3,8,256]{2,1,0:T(8,128)S(1)} %pad_maximum_fusion.1), channel_id=1, source_target_pairs={{0,48},{1,209},{2,50},{3,211},{4,52},{5,213},{6,54},{7,215},{8,56}... | collective-permute-start | bytes 73736 | tf_op jit(solution)/shard_map/ppermute | solution.py:172
  38.3 12.1 %collective-permute-start.4 = (f32[3,8,256]{2,1,0:T(8,128)S(1)}, f32[3,8,256]{2,1,0:T(8,128)S(1)}, u32[]{:S(2)}, u32[]{:S(2)}) collective-permute-start(f32[3,8,256]{2,1,0:T(8,128)S(1)} %collective-permute-done.3), channel_id=1, source_target_pairs={{0,1},{1,0},{2,3},{3,2},{4,5},{5,4},{6,7},{7,6},{8,9},{9,8},{10,11... | collective-permute-start | bytes 73736 | tf_op jit(solution)/shard_map/ppermute | solution.py:175
  38.6 1.8 %copy-start.1 = (f32[16,1,8,256]{3,2,1,0:T(8,128)S(1)}, f32[16,1,8,256]{3,2,1,0:T(8,128)}, u32[]{:S(2)}) copy-start(f32[16,1,8,256]{3,2,1,0:T(8,128)} %param.6) | copy-start | bytes 393220
  38.6 1.8 %copy-start.2 = (f32[16,1,8,256]{3,2,1,0:T(8,128)S(1)}, f32[16,1,8,256]{3,2,1,0:T(8,128)}, u32[]{:S(2)}) copy-start(f32[16,1,8,256]{3,2,1,0:T(8,128)} %param.7) | copy-start | bytes 393220
  43.0 20.1 %all-to-all-start.1 = ((f32[16,3,8,256]{3,2,1,0:T(8,128)}), f32[16,3,8,256]{3,2,1,0:T(8,128)S(1)}, u32[]{:S(2)}, u32[]{:S(2)}) async-start(f32[16,3,8,256]{3,2,1,0:T(8,128)} %shard_map.79), calls=%async_computation.1 | async-start | bytes 786432 | tf_op jit(solution)/shard_map/all_to_all | solution.py:222
  50.5 4.7 %collective-permute-start.5 = (f32[7,8,256]{2,1,0:T(8,128)S(1)}, f32[7,8,256]{2,1,0:T(8,128)S(1)}, u32[]{:S(2)}, u32[]{:S(2)}) collective-permute-start(f32[7,8,256]{2,1,0:T(8,128)S(1)} %slice.22), channel_id=1, source_target_pairs={{0,128},{1,129},{2,130},{3,131},{4,132},{5,133},{6,134},{7,135},{8... | collective-permute-start | bytes 172040 | tf_op jit(solution)/shard_map/ppermute | solution.py:172

commit v7 on v6

--- a/solution.py
+++ b/solution.py
@@ -108,11 +108,10 @@
         residual = got[x, 0] - image
         first = residual * (1.0 / theta)
         out[x, 0] = residual
-        out[x, 1] = first
         remain[x] = residual
         direction[0, x] = first
     for step in range(STEPS):
-        now, later = step % 2, (step + 1) % 2
+        now, later = step, step + 1
         rho_next = 1.0 / (2.0 * sigma - rho)
         flux_x = faces[planes - 1, 0] * (direction[now, planes - 1] - direction[now, 0])
         for x in range(planes):
@@ -126,8 +125,13 @@
             left = remain[x] - applied
             remain[x] = left
             new = (rho_next * rho) * value + (2.0 * rho_next / delta) * left
-            direction[later, x] = new
-            out[x, 1] = out[x, 1] + new
+            if step < STEPS - 1:
+                direction[later, x] = new
+            else:
+                total = direction[0, x]
+                for past in range(1, STEPS):
+                    total = total + direction[past, x]
+                out[x, 1] = total + new
         rho = rho_next
 
 
@@ -222,7 +226,7 @@
     got = lax.all_to_all(mixed, "gx", 0, 0, tiled=True)
     done = kernel_of(
         cheb_kernel, f32(planes, 2, *tile), [VMEM] * 3,
-        [VMEM((planes,) + tile, jnp.float32), VMEM((planes, 3) + tile, jnp.float32), VMEM((2, planes) + tile, jnp.float32), VMEM((planes,) + tile, jnp.float32)],
+        [VMEM((planes,) + tile, jnp.float32), VMEM((planes, 3) + tile, jnp.float32), VMEM((STEPS, planes) + tile, jnp.float32), VMEM((planes,) + tile, jnp.float32)],
         flops=planes * STEPS * 30 * cell, size=4 * cell * planes * 6,
     )(got, nine, rest)
     back = lax.all_to_all(done, "gx", 0, 0, tiled=True)

time: 79.7 us -> 79.7 us (level)
  no operation moved by 1% of the time
where the time goes in v7:
time: 79.7 us; the launch traced here: 79.2 us
  waiting for transfers between devices  35.2 us (44%)
  starting transfers between devices  20.1 us (25%)
  blocking collectives  14.8 us (19%)
  Pallas kernels  5.06 us (6%)
  local copies, waits for them, and re-layouts  2.85 us (4%)
  between operations  0.84 us (1%)
    all_to_all x1, waiting for transfers between devices, step(): lax.all_to_all(spread, 'ma', 0, 0, tiled=True, axis_index_groups=same_core)  16.1 us
    all_to_all x1, blocking collectives, step(): back = lax.all_to_all(done, 'gx', 0, 0, tiled=True)  14.8 us
    ppermute x3, waiting for transfers between devices, shifted(): return lax.ppermute(array, ('gx', 'ma'), pairs)  9.19 us
    all_to_all x1, waiting for transfers between devices, step(): got = lax.all_to_all(mixed, 'gx', 0, 0, tiled=True)  7.88 us
    all_to_all x1, starting transfers between devices, step(): got = lax.all_to_all(mixed, 'gx', 0, 0, tiled=True)  7.47 us
    all_to_all x1, starting transfers between devices, step(): lax.all_to_all(spread, 'ma', 0, 0, tiled=True, axis_index_groups=same_core)  6.16 us
    ppermute x3, starting transfers between devices, shifted(): return lax.ppermute(array, ('gx', 'ma'), pairs)  5.91 us
    pallas_call x1, Pallas kernels, step(): kernel_of(far_kernel, f32(modes, 3, *tile), [SMEM] * 2 + [VMEM] * 5, [VME...  2.49 us
  transfers between devices with their start and end apart: 8, of which 5 were waited for; matrix products, arithmetic and copies ran while one was open for 1% of the time, Pallas kernels for 6%

profile of v7, /device:TPU:2, one launch (start us, length us, event | category | flops | bytes accessed | tf_op | source)
XLA Modules:
  0.0 79.2 jit_solution(12058702170732966896)
XLA Ops:
  0.6 0.0 copy-start
  0.6 2.0 %broadcast_in_dim.17 = f32[8,16,8,256]{3,2,1,0:T(8,128)} broadcast(f32[16,8,256]{2,1,0:T(8,128)} %bitcast.17), dimensions={1,2,3} | broadcast | bytes 1179648 | tf_op jit(solution)/shard_map/broadcast_in_dim | solution.py:188
  2.6 6.2 %all-to-all-start = ((f32[8,16,8,256]{3,2,1,0:T(8,128)}), f32[8,16,8,256]{3,2,1,0:T(8,128)S(1)}, u32[]{:S(2)}, u32[]{:S(2)}) async-start(f32[8,16,8,256]{3,2,1,0:T(8,128)} %broadcast_in_dim.17), calls=%async_computation | async-start | bytes 2097152 | tf_op jit(solution)/shard_map/all_to_all | solution.py:189
  8.8 2.0 %collective-permute-start.1 = (f32[11,8,256]{2,1,0:T(8,128)S(1)}, f32[11,8,256]{2,1,0:T(8,128)S(1)}, u32[]{:S(2)}, u32[]{:S(2)}) collective-permute-start(f32[11,8,256]{2,1,0:T(8,128)S(1)} %pad_maximum_fusion.mid), channel_id=1, source_target_pairs={{0,16},{1,241},{2,18},{3,243},{4,20},{5,245},{6,22},{7,247},{8,24}... | collective-permute-start | bytes 270344 | tf_op jit(solution)/shard_map/ppermute | solution.py:176
  10.8 0.1 dynamic-slice_bitcast_fusion
  10.9 16.1 %all-to-all-done = f32[8,16,8,256]{3,2,1,0:T(8,128)S(1)} async-done(((f32[8,16,8,256]{3,2,1,0:T(8,128)}), f32[8,16,8,256]{3,2,1,0:T(8,128)S(1)}, u32[]{:S(2)}, u32[]{:S(2)}) %all-to-all-start) | async-done | bytes 1048608 | tf_op jit(solution)/shard_map/all_to_all | solution.py:189
  27.0 0.6 collective-permute-start.2
  27.6 0.1 bitcast_select_fusion.1
  27.7 2.1 %collective-permute-done.2.theirs = f32[11,8,256]{2,1,0:T(8,128)S(1)} collective-permute-done((f32[11,8,256]{2,1,0:T(8,128)S(1)}, f32[11,8,256]{2,1,0:T(8,128)S(1)}, u32[]{:S(2)}, u32[]{:S(2)}) %collective-permute-start.2) | collective-permute-done | bytes 90144 | tf_op jit(solution)/shard_map/ppermute | solution.py:179
  29.8 3.7 %collective-permute-start.3 = (f32[3,8,256]{2,1,0:T(8,128)S(1)}, f32[3,8,256]{2,1,0:T(8,128)S(1)}, u32[]{:S(2)}, u32[]{:S(2)}) collective-permute-start(f32[3,8,256]{2,1,0:T(8,128)S(1)} %pad_maximum_fusion.1), channel_id=1, source_target_pairs={{0,48},{1,209},{2,50},{3,211},{4,52},{5,213},{6,54},{7,215},{8,56}... | collective-permute-start | bytes 73736 | tf_op jit(solution)/shard_map/ppermute | solution.py:176
  33.5 0.1 bitcast_select_fusion.2
  33.6 4.7 %collective-permute-done.3 = f32[3,8,256]{2,1,0:T(8,128)S(1)} collective-permute-done((f32[3,8,256]{2,1,0:T(8,128)S(1)}, f32[3,8,256]{2,1,0:T(8,128)S(1)}, u32[]{:S(2)}, u32[]{:S(2)}) %collective-permute-start.3) | collective-permute-done | bytes 24608 | tf_op jit(solution)/shard_map/ppermute | solution.py:176
  38.3 0.1 add_bitcast_fusion
  38.4 0.2 shard_map.77.faces
  38.6 0.0 copy-start.1
  38.6 1.8 %shard_map.78.sums = f32[16,6,8,256]{3,2,1,0:T(8,128)S(1)} custom-call(s32[20,16]{1,0:T(8,128)S(1)} %reshape.21.index, f32[20,16]{1,0:T(8,128)S(1)} %reshape.24.weight, f32[128,8,256]{2,1,0:T(8,128)S(1)} %bitcast.15, f32[11,6,8,256]{3,2,1,0:T(8,128)S(1)} %shard_map.77.faces), custom_call_target="tpu_custom_call" | custom-call | flops 5767168 | bytes 2637824 | tf_op jit(solution)/shard_map/pallas_call | solution.py:210
  40.5 2.5 %shard_map.79 = f32[16,3,8,256]{3,2,1,0:T(8,128)} custom-call(s32[20,16]{1,0:T(8,128)S(1)} %reshape.21.index, f32[20,16]{1,0:T(8,128)S(1)} %reshape.22.weight, f32[128,8,256]{2,1,0:T(8,128)S(1)} %bitcast.16, f32[16,8,256]{2,1,0:T(8,128)S(1)} %bitcast.18, f32[16,8,256]{2,1,0:T(8,128)S(1)} %bitcast.19, f32[16,6,8,256]{3,2,1,0:T(8,128)S(1)} %shard_map.78.sums, ...), custom_call_target="tpu_custom_call" | custom-call | flops 5767168 | bytes 3031040 | tf_op jit(solution)/shard_map/pallas_call | solution.py:214
  43.0 7.5 %all-to-all-start.1 = ((f32[16,3,8,256]{3,2,1,0:T(8,128)}), f32[16,3,8,256]{3,2,1,0:T(8,128)S(1)}, u32[]{:S(2)}, u32[]{:S(2)}) async-start(f32[16,3,8,256]{3,2,1,0:T(8,128)} %shard_map.79), calls=%async_computation.1 | async-start | bytes 786432 | tf_op jit(solution)/shard_map/all_to_all | solution.py:226
  50.5 0.2 collective-permute-start.5
  50.7 4.5 %collective-permute-done.5.far_mean = f32[7,8,256]{2,1,0:T(8,128)S(1)} collective-permute-done((f32[7,8,256]{2,1,0:T(8,128)S(1)}, f32[7,8,256]{2,1,0:T(8,128)S(1)}, u32[]{:S(2)}, u32[]{:S(2)}) %collective-permute-start.5) | collective-permute-done | bytes 57376 | tf_op jit(solution)/shard_map/ppermute | solution.py:176
  55.2 7.9 %all-to-all-done.1.got = f32[16,3,8,256]{3,2,1,0:T(8,128)S(1)} async-done(((f32[16,3,8,256]{3,2,1,0:T(8,128)}), f32[16,3,8,256]{3,2,1,0:T(8,128)S(1)}, u32[]{:S(2)}, u32[]{:S(2)}) %all-to-all-start.1) | async-done | bytes 393248 | tf_op jit(solution)/shard_map/all_to_all | solution.py:226
  63.1 0.6 shard_map.80
  63.7 14.8 %all_to_all.15 = f32[16,2,8,256]{3,2,1,0:T(8,128)S(1)} all-to-all(f32[16,2,8,256]{3,2,1,0:T(8,128)S(1)} %shard_map.80), channel_id=1, replica_groups=mesh['gx'=16,'ma'=16] {'gx'}, dimensions={0} | all-to-all | bytes 524288 | tf_op jit(solution)/shard_map/all_to_all | solution.py:232
  78.5 0.7 fusion
  (29 shorter events, 0.1 us)
Async XLA Ops:
  0.6 10.2 %copy-start = (s32[256,10]{0,1:T(8,128)S(1)}, s32[256,10]{0,1:T(8,128)}, u32[]{:S(2)}) copy-start(s32[256,10]{0,1:T(8,128)} %param.11) | copy-start | bytes 30724
  2.6 6.2 %copy-start.3 = (f32[10,1,8,256]{3,2,1,0:T(8,128)S(1)}, f32[10,1,8,256]{3,2,1,0:T(8,128)}, u32[]{:S(2)}) copy-start(f32[10,1,8,256]{3,2,1,0:T(8,128)} %param.9) | copy-start | bytes 245764
  2.6 6.2 %copy-start.4 = (f32[1,8,256]{2,1,0:T(8,128)S(1)}, f32[1,8,256]{2,1,0:T(8,128)}, u32[]{:S(2)}) copy-start(f32[1,8,256]{2,1,0:T(8,128)} %param.8) | copy-start | bytes 24580
  2.6 24.3 %all-to-all-start = ((f32[8,16,8,256]{3,2,1,0:T(8,128)}), f32[8,16,8,256]{3,2,1,0:T(8,128)S(1)}, u32[]{:S(2)}, u32[]{:S(2)}) async-start(f32[8,16,8,256]{3,2,1,0:T(8,128)} %broadcast_in_dim.17), calls=%async_computation | async-start | bytes 2097152 | tf_op jit(solution)/shard_map/all_to_all | solution.py:189
  8.8 18.2 %collective-permute-start.1 = (f32[11,8,256]{2,1,0:T(8,128)S(1)}, f32[11,8,256]{2,1,0:T(8,128)S(1)}, u32[]{:S(2)}, u32[]{:S(2)}) collective-permute-start(f32[11,8,256]{2,1,0:T(8,128)S(1)} %pad_maximum_fusion.mid), channel_id=1, source_target_pairs={{0,16},{1,241},{2,18},{3,243},{4,20},{5,245},{6,22},{7,247},{8,24}... | collective-permute-start | bytes 270344 | tf_op jit(solution)/shard_map/ppermute | solution.py:176
  10.8 16.8 %copy-start.5 = (s32[10,256,2]{1,2,0:T(2,128)S(1)}, s32[10,256,2]{1,2,0:T(2,128)}, u32[]{:S(2)}) copy-start(s32[10,256,2]{1,2,0:T(2,128)} %param.10) | copy-start | bytes 61444
  27.0 13.5 %collective-permute-start = (f32[8,16,8,256]{3,2,1,0:T(8,128)S(1)}, f32[8,16,8,256]{3,2,1,0:T(8,128)S(1)}, u32[]{:S(2)}, u32[]{:S(2)}) collective-permute-start(f32[8,16,8,256]{3,2,1,0:T(8,128)S(1)} %all-to-all-done), channel_id=1, source_target_pairs={{0,1},{1,0},{2,3},{3,2},{4,5},{5,4},{6,7},{7,6},{8,9},{9,8},{10,11... | collective-permute-start | bytes 3145736 | tf_op jit(solution)/shard_map/ppermute | solution.py:179
  27.0 2.8 %collective-permute-start.2 = (f32[11,8,256]{2,1,0:T(8,128)S(1)}, f32[11,8,256]{2,1,0:T(8,128)S(1)}, u32[]{:S(2)}, u32[]{:S(2)}) collective-permute-start(f32[11,8,256]{2,1,0:T(8,128)S(1)} %collective-permute-done.1.mine), channel_id=1, source_target_pairs={{0,1},{1,0},{2,3},{3,2},{4,5},{5,4},{6,7},{7,6},{8,9},{9,8},{10,11... | collective-permute-start | bytes 270344 | tf_op jit(solution)/shard_map/ppermute | solution.py:179
  29.8 8.5 %collective-permute-start.3 = (f32[3,8,256]{2,1,0:T(8,128)S(1)}, f32[3,8,256]{2,1,0:T(8,128)S(1)}, u32[]{:S(2)}, u32[]{:S(2)}) collective-permute-start(f32[3,8,256]{2,1,0:T(8,128)S(1)} %pad_maximum_fusion.1), channel_id=1, source_target_pairs={{0,48},{1,209},{2,50},{3,211},{4,52},{5,213},{6,54},{7,215},{8,56}... | collective-permute-start | bytes 73736 | tf_op jit(solution)/shard_map/ppermute | solution.py:176
  38.3 12.1 %collective-permute-start.4 = (f32[3,8,256]{2,1,0:T(8,128)S(1)}, f32[3,8,256]{2,1,0:T(8,128)S(1)}, u32[]{:S(2)}, u32[]{:S(2)}) collective-permute-start(f32[3,8,256]{2,1,0:T(8,128)S(1)} %collective-permute-done.3), channel_id=1, source_target_pairs={{0,1},{1,0},{2,3},{3,2},{4,5},{5,4},{6,7},{7,6},{8,9},{9,8},{10,11... | collective-permute-start | bytes 73736 | tf_op jit(solution)/shard_map/ppermute | solution.py:179
  38.6 1.8 %copy-start.1 = (f32[16,1,8,256]{3,2,1,0:T(8,128)S(1)}, f32[16,1,8,256]{3,2,1,0:T(8,128)}, u32[]{:S(2)}) copy-start(f32[16,1,8,256]{3,2,1,0:T(8,128)} %param.6) | copy-start | bytes 393220
  38.6 1.8 %copy-start.2 = (f32[16,1,8,256]{3,2,1,0:T(8,128)S(1)}, f32[16,1,8,256]{3,2,1,0:T(8,128)}, u32[]{:S(2)}) copy-start(f32[16,1,8,256]{3,2,1,0:T(8,128)} %param.7) | copy-start | bytes 393220
  43.0 20.1 %all-to-all-start.1 = ((f32[16,3,8,256]{3,2,1,0:T(8,128)}), f32[16,3,8,256]{3,2,1,0:T(8,128)S(1)}, u32[]{:S(2)}, u32[]{:S(2)}) async-start(f32[16,3,8,256]{3,2,1,0:T(8,128)} %shard_map.79), calls=%async_computation.1 | async-start | bytes 786432 | tf_op jit(solution)/shard_map/all_to_all | solution.py:226
  50.5 4.7 %collective-permute-start.5 = (f32[7,8,256]{2,1,0:T(8,128)S(1)}, f32[7,8,256]{2,1,0:T(8,128)S(1)}, u32[]{:S(2)}, u32[]{:S(2)}) collective-permute-start(f32[7,8,256]{2,1,0:T(8,128)S(1)} %slice.22), channel_id=1, source_target_pairs={{0,128},{1,129},{2,130},{3,131},{4,132},{5,133},{6,134},{7,135},{8... | collective-permute-start | bytes 172040 | tf_op jit(solution)/shard_map/ppermute | solution.py:176
